TPU v7x, 256 devices: a whole 4x4x8 slice. The times are simulated.
256 devices in a mesh: rows: 16 (over x, y), cols: 16 (over z, core).
Axes of the slice: x: 4, y: 4, z: 8, core: 2. Of those that a mesh axis runs over, the one named last changes fastest.
Arguments:
- power: float32 [2, 4, 2048, 2048], P(None, None, 'rows', 'cols'), may hold values from -6 to 6
- material: int32 [4, 2048, 2048], P(None, 'rows', 'cols'), may hold values from 0 to 7
- cond_table: float32 [4, 8], replicated, may hold values from 0.5 to 8
- tier_table: int32 [4], replicated, may hold values from 0 to 3
- coarse_slot: int32 [256], replicated, may hold values from 0 to 255, each once
- coarse_inverse: float32 [16, 16, 16], replicated, as said below
Outputs:
- solution: float32 [2, 4, 2048, 2048], P(None, None, 'rows', 'cols')
- residual: float32 [2, 4, 2048, 2048], P(None, None, 'rows', 'cols')
- precond: float32 [2, 4, 2048, 2048], P(None, None, 'rows', 'cols')
Inputs may be any that keep to these rules, and one draw needn't show every extreme that they name: `coarse_slot`: each value once. `coarse_inverse`: symmetric within each owner.
All inputs are finite; a program needn't handle non-finite values.
Results may differ from a plain program's by a relative error of at most 0.0003.
Values sent between devices are 32-bit elements; how exact they have to be, the bound alone decides.
No kernel may reach another device: no remote copies, remote signals or barrier semaphores. Data moves between devices by JAX's collectives and lax.ppermute only.
A program may use at most 64 MiB of HBM per device.

v0:
```python
import math

import jax
import jax.numpy as jnp
from jax import lax
from jax.sharding import PartitionSpec as P

SUB = 128
TIERS = 4
ITERS = 2


SHIFT_C = 0.5
VERT_C = 2.0
SINK_C = 0.05
HIGH = lax.Precision.HIGHEST


def with_halo(cells, sides, width):
    for axis, dim in sides:
        count = lax.axis_size(axis)
        ends = count - 1
        head = lax.slice_in_dim(cells, 0, width, axis=dim)
        tail = lax.slice_in_dim(cells, cells.shape[dim] - width, cells.shape[dim], axis=dim)
        cells = jnp.concatenate(
            [
                lax.ppermute(tail, axis, [(i, (i + 1) % count) for i in range(ends)]),
                cells,
                lax.ppermute(head, axis, [((i + 1) % count, i) for i in range(ends)]),
            ],
            axis=dim,
        )
    return cells


def sine_basis(length):
    counting = jnp.arange(1, length + 1).astype(jnp.float32)
    step_angle = math.pi / (length + 1)
    basis = math.sqrt(2.0 / (length + 1)) * jnp.sin(
        step_angle * counting[:, None] * counting[None, :]
    )
    eigen_values = 2.0 - 2.0 * jnp.cos(step_angle * counting)
    return (basis, eigen_values)


def conductivity(material, cond_table, tier_table):
    tables = cond_table.shape[0]
    picker = (tier_table[:, None] == jnp.arange(tables, dtype=jnp.int32)[None, :]).astype(
        jnp.float32
    )
    tier_rows = jnp.dot(picker, cond_table, precision=HIGH)
    cond = jnp.zeros(material.shape, jnp.float32)
    for number in range(cond_table.shape[1]):
        cond = cond + jnp.where(material == number, tier_rows[:, number][:, None, None], 0.0)
    return (cond, jnp.mean(tier_rows, axis=1))


def coefficients(cond, padded):
    north = 0.5 * (cond + padded[:, :-2, 1:-1])
    south = 0.5 * (cond + padded[:, 2:, 1:-1])
    west = 0.5 * (cond + padded[:, 1:-1, :-2])
    east = 0.5 * (cond + padded[:, 1:-1, 2:])
    upward = VERT_C * 0.5 * (cond[:-1] + cond[1:])
    sink = jnp.concatenate([SINK_C * cond[:1], jnp.zeros_like(cond[1:])], 0)
    return (north, south, west, east, upward, sink)


def operate(temps, padded, coefs):
    north, south, west, east, upward, sink = coefs
    lateral = north * (temps - padded[:, :, :-2, 1:-1]) + south * (temps - padded[:, :, 2:, 1:-1])
    lateral = (
        lateral + west * (temps - padded[:, :, 1:-1, :-2]) + east * (temps - padded[:, :, 1:-1, 2:])
    )
    flux = upward * (temps[:, :-1] - temps[:, 1:])
    zeros_tier = jnp.zeros_like(temps[:, :1])
    vertical = jnp.concatenate([flux, zeros_tier], 1) - jnp.concatenate([zeros_tier, flux], 1)
    return lateral + vertical + sink * temps


def block_solve(temps, basis, denominator):
    shape = temps.shape
    length = basis.shape[0]
    blocks = temps.reshape(
        shape[0], shape[1], shape[2] // length, length, shape[3] // length, length
    )
    spectral = jnp.einsum("ia,vtxayb->vtxiyb", basis, blocks, precision=HIGH)
    spectral = jnp.einsum("vtxiyb,bj->vtxiyj", spectral, basis, precision=HIGH)
    spectral = spectral / denominator[None, :, None, :, None, :]
    result = jnp.einsum("ia,vtxayb->vtxiyb", basis, spectral, precision=HIGH)
    result = jnp.einsum("vtxiyb,bj->vtxiyj", result, basis, precision=HIGH)
    return result.reshape(shape)


def pad_rim(values):
    return with_halo(values, (("rows", 2), ("cols", 3)), 1)


def inner_local(left_arr, right_arr):
    return jnp.sum(left_arr * right_arr, axis=(1, 2, 3))


def shards(power, material, cond_table, tier_table, coarse_slot, coarse_inverse):
    cond, mean_cond = conductivity(material, cond_table, tier_table)
    coefs = coefficients(cond, pad_rim(cond[None])[0])
    basis, eigen_values = sine_basis(SUB)
    denominator = mean_cond[:, None, None] * (
        eigen_values[:, None] + eigen_values[None, :] + SHIFT_C
    )
    half = SUB // 2
    scale = 1.0 / math.sqrt(SUB * SUB * TIERS)
    tile = power.shape[2]
    blocks_side = tile // SUB
    total = coarse_slot.shape[0]
    row_index = lax.axis_index("rows")
    col_index = lax.axis_index("cols")
    row_ids = row_index * blocks_side + jnp.arange(blocks_side, dtype=jnp.int32)
    col_ids = col_index * blocks_side + jnp.arange(blocks_side, dtype=jnp.int32)
    global_ids = (
        row_ids[:, None] * (lax.axis_size("cols") * blocks_side) + col_ids[None, :]
    ).reshape(-1)
    columns = jnp.arange(total, dtype=jnp.int32)
    local_slot = jnp.sum(
        jnp.where(global_ids[:, None] == columns[None, :], coarse_slot[None, :], 0), axis=1
    )
    placer = (local_slot[:, None] == columns[None, :]).astype(jnp.float32)
    owners = coarse_inverse.shape[0]
    own_count = coarse_inverse.shape[1]

    def precondition(resid):
        variants = resid.shape[0]
        aligned = block_solve(resid, basis, denominator)
        extended = with_halo(resid, (("rows", 2), ("cols", 3)), half)
        positions = jnp.arange(tile + SUB, dtype=jnp.int32)
        mask_rows = jnp.where((positions < SUB) & (row_index == 0), 0.0, 1.0)
        mask_cols = jnp.where((positions < SUB) & (col_index == 0), 0.0, 1.0)
        solved_ext = (
            block_solve(extended, basis, denominator) * mask_rows[:, None] * mask_cols[None, :]
        )
        offset = solved_ext[:, :, half : half + tile, half : half + tile]
        sums = (
            resid.reshape(variants, TIERS, blocks_side, SUB, blocks_side, SUB).sum(axis=(1, 3, 5))
            * scale
        )
        ordered = jnp.einsum(
            "sc,vs->cv", placer, sums.reshape(variants, blocks_side * blocks_side), precision=HIGH
        )
        stacked = ordered.reshape(owners, own_count, variants)
        owned = lax.psum_scatter(stacked, "cols", scatter_dimension=0, tiled=True)
        owned = lax.psum(owned, "rows")
        mine = lax.dynamic_slice_in_dim(coarse_inverse, col_index, 1, 0)
        own_sol = jnp.einsum("okj,ojv->okv", mine, owned, precision=HIGH)
        every_sol = lax.all_gather(own_sol, "cols", axis=0, tiled=True)
        picked = jnp.einsum("sc,cv->vs", placer, every_sol.reshape(total, variants), precision=HIGH)
        picked = picked.reshape(variants, 1, blocks_side, 1, blocks_side, 1)
        coarse = jnp.broadcast_to(picked, (variants, TIERS, blocks_side, SUB, blocks_side, SUB))
        return aligned + offset + coarse.reshape(resid.shape) * scale

    solution = jnp.zeros_like(power)
    residual = power
    precond = precondition(residual)
    direction = precond

    def rz_sum(left_arr, right_arr):
        return lax.psum(inner_local(left_arr, right_arr), ("rows", "cols"))

    rz_now = rz_sum(residual, precond)
    for number in range(ITERS):
        image = operate(direction, pad_rim(direction), coefs)
        alpha = rz_now / lax.psum(inner_local(direction, image), ("rows", "cols"))
        solution = solution + alpha[:, None, None, None] * direction
        residual = residual - alpha[:, None, None, None] * image
        precond = precondition(residual)
        rz_next = rz_sum(residual, precond)
        direction = precond + (rz_next / rz_now)[:, None, None, None] * direction
        rz_now = rz_next
    return (solution, residual, precond)


def solution(mesh):
    in_specs = (P(None, None, "rows", "cols"), P(None, "rows", "cols"), P(), P(), P(), P())
    out_specs = (
        P(None, None, "rows", "cols"),
        P(None, None, "rows", "cols"),
        P(None, None, "rows", "cols"),
    )
    return jax.shard_map(shards, mesh=mesh, in_specs=in_specs, out_specs=out_specs, check_vma=False)
```

profile of v0, /device:TPU:1, one launch (start us, length us, event | category | flops | bytes accessed | tf_op | source)
XLA Modules:
  0.0 762.5 jit_solution(1685460788034805416)
XLA Ops:
  4.4 4.7 collective-permute-start
  12.0 4.0 collective-permute-start.4
  18.7 48.1 %all-reduce.5 = f32[16,16,2]{1,2,0:T(2,128)S(1)} all-reduce(f32[16,16,2]{1,2,0:T(2,128)S(1)} %broadcast_multiply_fusion.3), channel_id=5, replica_groups=mesh['rows'=16,'cols'=16] {'cols'}, use_global_device_ids=true, to_apply=%region_3.4.clone | all-reduce | flops 512 | bytes 4096
  68.2 32.1 %psum.49 = f32[16,2]{0,1:T(2,128)S(1)} all-reduce(f32[16,2]{0,1:T(2,128)S(1)} %dynamic-slice_bitcast_fusion.2), channel_id=1, replica_groups=mesh['rows'=16,'cols'=16] {'rows'}, use_global_device_ids=true, to_apply=%region_4.5 | all-reduce | flops 32 | bytes 256 | tf_op jit(solution)/shard_map/psum | solution.py:149
  100.5 24.5 %all-gather.3 = f32[16,16,2]{1,2,0:T(2,128)S(1)} all-gather(f32[1,16,2]{1,2,0:T(2,128)S(1)} %convolution_bitcast_fusion.8), channel_id=2, replica_groups=mesh['rows'=16,'cols'=16] {'cols'}, dimensions={0}, use_global_device_ids=true | all-gather | bytes 2176 | tf_op jit(solution)/shard_map/all_gather | solution.py:152
  133.0 3.5 collective-permute-start.2
  139.8 3.6 collective-permute-start.6
  149.7 2.5 reshape.355
  154.4 3.6 fusion.10
  158.0 3.8 fusion.22
  161.7 4.1 fusion.8
  167.5 2.7 reshape.316
  170.2 2.6 fusion.26
  174.1 4.0 collective-permute-start.8
  185.6 5.0 collective-permute-start.10
  195.7 78.5 %all-reduce.8 = (f32[2]{0:T(128)S(1)}, f32[2]{0:T(128)S(1)}) all-reduce(f32[2]{0:T(128)S(1)} %get-tuple-element.4, f32[2]{0:T(128)S(1)} %get-tuple-element.3), channel_id=1, replica_groups=mesh['rows'=16,'cols'=16] {'rows','cols'}, use_global_device_ids=true, to_apply=%region_6.7 | all-reduce | flops 4 | bytes 32 | tf_op jit(solution)/shard_map/psum | solution.py:164
  275.4 44.4 %all-reduce.6 = f32[16,16,2]{1,2,0:T(2,128)S(1)} all-reduce(f32[16,16,2]{1,2,0:T(2,128)S(1)} %broadcast_multiply_fusion.2), channel_id=6, replica_groups=mesh['rows'=16,'cols'=16] {'cols'}, use_global_device_ids=true, to_apply=%region_10.11.clone | all-reduce | flops 512 | bytes 4096
  320.5 29.8 %psum.52 = f32[16,2]{0,1:T(2,128)S(1)} all-reduce(f32[16,2]{0,1:T(2,128)S(1)} %dynamic-slice_bitcast_fusion.1), channel_id=1, replica_groups=mesh['rows'=16,'cols'=16] {'rows'}, use_global_device_ids=true, to_apply=%region_11.12 | all-reduce | flops 32 | bytes 256 | tf_op jit(solution)/shard_map/psum | solution.py:149
  351.6 4.0 collective-permute-start.12
  355.8 25.2 %all-gather.4 = f32[16,16,2]{1,2,0:T(2,128)S(1)} all-gather(f32[1,16,2]{1,2,0:T(2,128)S(1)} %convolution_bitcast_fusion.7), channel_id=3, replica_groups=mesh['rows'=16,'cols'=16] {'cols'}, dimensions={0}, use_global_device_ids=true | all-gather | bytes 2176 | tf_op jit(solution)/shard_map/all_gather | solution.py:152
  390.0 3.5 collective-permute-start.14
  402.3 3.5 pad_maximum_fusion.1
  405.8 3.4 reshape.323
  409.3 5.2 fusion.16
  414.5 3.6 fusion.6
  418.1 3.8 fusion.20
  421.9 4.1 fusion.4
  426.0 3.0 copy.104
  429.0 3.9 reshape.324
  432.9 2.5 multiply_reduce_fusion.1
  435.4 74.4 %psum.53 = f32[2]{0:T(128)S(1)} all-reduce(f32[2]{0:T(128)S(1)} %get-tuple-element.53), channel_id=1, replica_groups=mesh['rows'=16,'cols'=16] {'rows','cols'}, use_global_device_ids=true, to_apply=%region_13.14 | all-reduce | flops 2 | bytes 16 | tf_op jit(solution)/shard_map/psum | solution.py:164
  511.3 4.0 collective-permute-start.16
  518.8 3.7 collective-permute-start.19
  523.9 2.6 collective-permute-start.18
  529.5 2.8 multiply_reduce_fusion
  532.2 78.1 %psum.54 = f32[2]{0:T(128)S(1)} all-reduce(f32[2]{0:T(128)} %get-tuple-element.17), channel_id=1, replica_groups=mesh['rows'=16,'cols'=16] {'rows','cols'}, use_global_device_ids=true, to_apply=%region_15.16 | all-reduce | flops 2 | bytes 16 | tf_op jit(solution)/shard_map/psum | solution.py:169
  614.1 4.0 collective-permute-start.20
  618.2 44.4 %all-reduce.7 = f32[16,16,2]{1,2,0:T(2,128)S(1)} all-reduce(f32[16,16,2]{1,2,0:T(2,128)S(1)} %broadcast_multiply_fusion.1), channel_id=7, replica_groups=mesh['rows'=16,'cols'=16] {'cols'}, use_global_device_ids=true, to_apply=%region_17.18.clone | all-reduce | flops 512 | bytes 4096
  663.3 29.1 %psum.55 = f32[16,2]{0,1:T(2,128)S(1)} all-reduce(f32[16,2]{0,1:T(2,128)S(1)} %dynamic-slice_bitcast_fusion), channel_id=1, replica_groups=mesh['rows'=16,'cols'=16] {'rows'}, use_global_device_ids=true, to_apply=%region_18.19 | all-reduce | flops 32 | bytes 256 | tf_op jit(solution)/shard_map/psum | solution.py:149
  692.5 24.7 %all-gather.5 = f32[16,16,2]{1,2,0:T(2,128)S(1)} all-gather(f32[1,16,2]{1,2,0:T(2,128)S(1)} %convolution_bitcast_fusion.6), channel_id=4, replica_groups=mesh['rows'=16,'cols'=16] {'cols'}, dimensions={0}, use_global_device_ids=true | all-gather | bytes 2176 | tf_op jit(solution)/shard_map/all_gather | solution.py:152
  723.0 3.5 collective-permute-start.22
  734.0 3.2 pad_maximum_fusion.2
  739.7 3.7 fusion.14
  743.4 3.6 fusion.2
  747.0 3.8 fusion.18
  750.8 3.9 fusion
  756.3 2.7 reshape.331
  759.0 3.2 fusion.24
  (243 shorter events, 97.7 us)
Async XLA Ops:
  0.6 99.7 %copy-start = (f32[16,16,16]{2,1,0:T(8,128)S(1)}, f32[16,16,16]{2,1,0:T(8,128)}, u32[]{:S(2)}) copy-start(f32[16,16,16]{2,1,0:T(8,128)} %param.11) | copy-start | bytes 49156
  2.0 15.2 %copy-start.46 = (s32[256]{0:T(256)S(1)}, s32[256]{0:T(256)}, u32[]{:S(2)}) copy-start(s32[256]{0:T(256)} %param.10) | copy-start | bytes 3076
  2.0 16.5 %copy-start.1 = (f32[2,4,128,128]{3,2,1,0:T(8,128)S(1)}, f32[2,4,128,128]{3,2,1,0:T(8,128)}, u32[]{:S(2)}) copy-start(f32[2,4,128,128]{3,2,1,0:T(8,128)} %param.6) | copy-start | bytes 1572868
  2.0 64.9 %copy-start.49 = (u32[256]{0:T(256)S(1)}, u32[256]{0:T(256)}, u32[]{:S(2)}) copy-start(u32[256]{0:T(256)} %constant.68) | copy-start | bytes 3076
  3.1 127.2 %collective-permute-start.1 = (f32[2,4,64,128]{2,3,1,0:T(8,128)}, f32[2,4,64,128]{2,3,1,0:T(8,128)S(1)}, u32[]{:S(2)}, u32[]{:S(2)}) collective-permute-start(f32[2,4,64,128]{2,3,1,0:T(8,128)} %get-tuple-element.45), channel_id=1, source_target_pairs={{16,0},{32,16},{48,32},{64,48},{80,64},{96,80},{112,96},{128,112},... | collective-permute-start | bytes 786440 | tf_op jit(solution)/shard_map/ppermute | solution.py:29
  4.4 125.9 %collective-permute-start = (f32[2,4,64,128]{2,3,1,0:T(8,128)}, f32[2,4,64,128]{2,3,1,0:T(8,128)S(1)}, u32[]{:S(2)}, u32[]{:S(2)}) collective-permute-start(f32[2,4,64,128]{2,3,1,0:T(8,128)} %get-tuple-element.44), channel_id=1, source_target_pairs={{0,16},{16,32},{32,48},{48,64},{64,80},{80,96},{96,112},{112,128},... | collective-permute-start | bytes 786440 | tf_op jit(solution)/shard_map/ppermute | solution.py:27
  9.7 118.6 %copy-start.25 = (f32[4]{0:T(128)}, f32[4]{0:T(128)S(1)}, u32[]{:S(2)}) copy-start(f32[4]{0:T(128)S(1)} %get-tuple-element.5) | copy-start | bytes 52
  9.7 118.6 %copy-start.27 = (f32[4]{0:T(128)}, f32[4]{0:T(128)S(1)}, u32[]{:S(2)}) copy-start(f32[4]{0:T(128)S(1)} %get-tuple-element.6) | copy-start | bytes 52
  9.8 118.6 %copy-start.29 = (f32[4]{0:T(128)}, f32[4]{0:T(128)S(1)}, u32[]{:S(2)}) copy-start(f32[4]{0:T(128)S(1)} %get-tuple-element.7) | copy-start | bytes 52
  9.8 118.6 %copy-start.31 = (f32[4]{0:T(128)}, f32[4]{0:T(128)S(1)}, u32[]{:S(2)}) copy-start(f32[4]{0:T(128)S(1)} %get-tuple-element.8) | copy-start | bytes 52
  9.8 118.6 %copy-start.33 = (f32[4]{0:T(128)}, f32[4]{0:T(128)S(1)}, u32[]{:S(2)}) copy-start(f32[4]{0:T(128)S(1)} %get-tuple-element.9) | copy-start | bytes 52
  9.8 118.6 %copy-start.35 = (f32[4]{0:T(128)}, f32[4]{0:T(128)S(1)}, u32[]{:S(2)}) copy-start(f32[4]{0:T(128)S(1)} %get-tuple-element.10) | copy-start | bytes 52
  10.7 125.8 %collective-permute-start.5 = (f32[1,4,1,128]{3,2,1,0:T(1,128)}, f32[1,4,1,128]{3,2,1,0:T(1,128)S(1)}, u32[]{:S(2)}, u32[]{:S(2)}) collective-permute-start(f32[1,4,1,128]{3,2,1,0:T(1,128)} %get-tuple-element.49), channel_id=1, source_target_pairs={{16,0},{32,16},{48,32},{64,48},{80,64},{96,80},{112,96},{128,112},... | collective-permute-start | bytes 6152 | tf_op jit(solution)/shard_map/ppermute | solution.py:29
  12.0 124.5 %collective-permute-start.4 = (f32[1,4,1,128]{3,2,1,0:T(1,128)}, f32[1,4,1,128]{3,2,1,0:T(1,128)S(1)}, u32[]{:S(2)}, u32[]{:S(2)}) collective-permute-start(f32[1,4,1,128]{3,2,1,0:T(1,128)} %get-tuple-element.48), channel_id=1, source_target_pairs={{0,16},{16,32},{32,48},{48,64},{64,80},{80,96},{96,112},{112,128},... | collective-permute-start | bytes 6152 | tf_op jit(solution)/shard_map/ppermute | solution.py:27
  130.8 12.8 %copy-start.20 = (f32[1,128,128]{2,1,0:T(8,128)S(1)}, f32[1,128,128]{2,1,0:T(8,128)}, u32[]{:S(2)}) copy-start(f32[1,128,128]{2,1,0:T(8,128)} %slice_multiply_fusion.3) | copy-start | bytes 196612
  130.9 17.0 %collective-permute-start.3 = (f32[2,4,256,64]{2,3,1,0:T(8,128)S(1)}, f32[2,4,256,64]{2,3,1,0:T(8,128)S(1)}, u32[]{:S(2)}, u32[]{:S(2)}) collective-permute-start(f32[2,4,256,64]{2,3,1,0:T(8,128)S(1)} %get-tuple-element.27), channel_id=1, source_target_pairs={{1,0},{2,1},{3,2},{4,3},{5,4},{6,5},{7,6},{8,7},{9,8},{10,9},{11,1... | collective-permute-start | bytes 1572872 | tf_op jit(solution)/shard_map/ppermute | solution.py:29
  133.0 14.9 %collective-permute-start.2 = (f32[2,4,256,64]{2,3,1,0:T(8,128)S(1)}, f32[2,4,256,64]{2,3,1,0:T(8,128)S(1)}, u32[]{:S(2)}, u32[]{:S(2)}) collective-permute-start(f32[2,4,256,64]{2,3,1,0:T(8,128)S(1)} %get-tuple-element.26), channel_id=1, source_target_pairs={{0,1},{1,2},{2,3},{3,4},{4,5},{5,6},{6,7},{7,8},{8,9},{9,10},{10,1... | collective-permute-start | bytes 1572872 | tf_op jit(solution)/shard_map/ppermute | solution.py:27
  137.8 7.9 %collective-permute-start.7 = (f32[1,4,130,1]{3,2,1,0:T(8,128)S(1)}, f32[1,4,130,1]{3,2,1,0:T(8,128)S(1)}, u32[]{:S(2)}, u32[]{:S(2)}) collective-permute-start(f32[1,4,130,1]{3,2,1,0:T(8,128)S(1)} %get-tuple-element.47), channel_id=1, source_target_pairs={{1,0},{2,1},{3,2},{4,3},{5,4},{6,5},{7,6},{8,7},{9,8},{10,9},{11,1... | collective-permute-start | bytes 6248 | tf_op jit(solution)/shard_map/ppermute | solution.py:29
  139.8 7.1 collective-permute-start.6
  143.5 26.7 %copy-start.39 = (f32[128]{0:T(128)}, f32[128]{0:T(128)S(1)}, u32[]{:S(2)}) copy-start(f32[128]{0:T(128)S(1)} %slice.230) | copy-start | bytes 1540
  143.6 26.6 %copy-start.42 = (f32[128]{0:T(128)}, f32[128]{0:T(128)S(1)}, u32[]{:S(2)}) copy-start(f32[128]{0:T(128)S(1)} %slice.229) | copy-start | bytes 1540
  172.8 6.8 collective-permute-start.9
  174.1 5.5 collective-permute-start.8
  179.5 14.0 %copy-start.4 = (f32[4,128,128]{2,1,0:T(8,128)}, f32[4,128,128]{2,1,0:T(8,128)S(1)}, u32[]{:S(2)}) copy-start(f32[4,128,128]{2,1,0:T(8,128)S(1)} %get-tuple-element.28) | copy-start | bytes 786436
  179.5 14.0 %copy-start.6 = (f32[4,128,128]{2,1,0:T(8,128)}, f32[4,128,128]{2,1,0:T(8,128)S(1)}, u32[]{:S(2)}) copy-start(f32[4,128,128]{2,1,0:T(8,128)S(1)} %get-tuple-element.29) | copy-start | bytes 786436
  179.5 13.9 %copy-start.8 = (f32[4,128,128]{2,1,0:T(8,128)}, f32[4,128,128]{2,1,0:T(8,128)S(1)}, u32[]{:S(2)}) copy-start(f32[4,128,128]{2,1,0:T(8,128)S(1)} %get-tuple-element.30) | copy-start | bytes 786436
  179.6 13.9 %copy-start.10 = (f32[4,128,128]{2,1,0:T(8,128)}, f32[4,128,128]{2,1,0:T(8,128)S(1)}, u32[]{:S(2)}) copy-start(f32[4,128,128]{2,1,0:T(8,128)S(1)} %get-tuple-element.31) | copy-start | bytes 786436
  180.8 12.7 %copy-start.3 = (f32[4,128,128]{2,1,0:T(8,128)S(1)}, f32[4,128,128]{2,1,0:T(8,128)}, u32[]{:S(2)}) copy-start(f32[4,128,128]{2,1,0:T(8,128)} %concatenate.82) | copy-start | bytes 786436
  182.3 9.1 %collective-permute-start.11 = (f32[2,4,130,1]{2,1,3,0:T(4,128)S(1)}, f32[2,4,130,1]{2,1,3,0:T(4,128)S(1)}, u32[]{:S(2)}, u32[]{:S(2)}) collective-permute-start(f32[2,4,130,1]{2,1,3,0:T(4,128)S(1)} %copy.90), channel_id=1, source_target_pairs={{1,0},{2,1},{3,2},{4,3},{5,4},{6,5},{7,6},{8,7},{9,8},{10,9},{11,1... | collective-permute-start | bytes 12488 | tf_op jit(solution)/shard_map/ppermute | solution.py:29
  185.6 6.8 collective-permute-start.10
  350.3 32.7 %collective-permute-start.13 = (f32[2,4,64,128]{3,2,1,0:T(8,128)S(1)}, f32[2,4,64,128]{3,2,1,0:T(8,128)S(1)}, u32[]{:S(2)}, u32[]{:S(2)}) collective-permute-start(f32[2,4,64,128]{3,2,1,0:T(8,128)S(1)} %get-tuple-element.41), channel_id=1, source_target_pairs={{16,0},{32,16},{48,32},{64,48},{80,64},{96,80},{112,96},{128,112},... | collective-permute-start | bytes 786440 | tf_op jit(solution)/shard_map/ppermute | solution.py:29
  351.6 31.4 %collective-permute-start.12 = (f32[2,4,64,128]{3,2,1,0:T(8,128)S(1)}, f32[2,4,64,128]{3,2,1,0:T(8,128)S(1)}, u32[]{:S(2)}, u32[]{:S(2)}) collective-permute-start(f32[2,4,64,128]{3,2,1,0:T(8,128)S(1)} %get-tuple-element.40), channel_id=1, source_target_pairs={{0,16},{16,32},{32,48},{48,64},{64,80},{80,96},{96,112},{112,128},... | collective-permute-start | bytes 786440 | tf_op jit(solution)/shard_map/ppermute | solution.py:27
  386.8 10.8 %collective-permute-start.15 = (f32[2,4,256,64]{2,3,1,0:T(8,128)}, f32[2,4,256,64]{2,3,1,0:T(8,128)}, u32[]{:S(2)}, u32[]{:S(2)}) collective-permute-start(f32[2,4,256,64]{2,3,1,0:T(8,128)} %copy.97), channel_id=1, source_target_pairs={{1,0},{2,1},{3,2},{4,3},{5,4},{6,5},{7,6},{8,7},{9,8},{10,9},{11,1... | collective-permute-start | bytes 1572872 | tf_op jit(solution)/shard_map/ppermute | solution.py:29
  390.0 9.9 %collective-permute-start.14 = (f32[2,4,256,64]{2,3,1,0:T(8,128)}, f32[2,4,256,64]{2,3,1,0:T(8,128)}, u32[]{:S(2)}, u32[]{:S(2)}) collective-permute-start(f32[2,4,256,64]{2,3,1,0:T(8,128)} %copy.96), channel_id=1, source_target_pairs={{0,1},{1,2},{2,3},{3,4},{4,5},{5,6},{6,7},{7,8},{8,9},{9,10},{10,1... | collective-permute-start | bytes 1572872 | tf_op jit(solution)/shard_map/ppermute | solution.py:27
  432.9 77.0 %copy-start.51 = (f32[2]{0:T(128)S(1)}, f32[2]{0:T(128)}, u32[]{:S(2)}) copy-start(f32[2]{0:T(128)} %copy-done.50) | copy-start | bytes 28
  510.0 5.3 collective-permute-start.17
  511.3 4.7 collective-permute-start.16
  517.3 12.2 %copy-start.5 = (f32[4,128,128]{2,1,0:T(8,128)S(1)}, f32[4,128,128]{2,1,0:T(8,128)}, u32[]{:S(2)}) copy-start(f32[4,128,128]{2,1,0:T(8,128)} %copy-done.4) | copy-start | bytes 786436
  517.3 12.2 %copy-start.7 = (f32[4,128,128]{2,1,0:T(8,128)S(1)}, f32[4,128,128]{2,1,0:T(8,128)}, u32[]{:S(2)}) copy-start(f32[4,128,128]{2,1,0:T(8,128)} %copy-done.6) | copy-start | bytes 786436
  517.3 12.2 %copy-start.9 = (f32[4,128,128]{2,1,0:T(8,128)S(1)}, f32[4,128,128]{2,1,0:T(8,128)}, u32[]{:S(2)}) copy-start(f32[4,128,128]{2,1,0:T(8,128)} %copy-done.8) | copy-start | bytes 786436
  517.3 12.2 %copy-start.11 = (f32[4,128,128]{2,1,0:T(8,128)S(1)}, f32[4,128,128]{2,1,0:T(8,128)}, u32[]{:S(2)}) copy-start(f32[4,128,128]{2,1,0:T(8,128)} %copy-done.10) | copy-start | bytes 786436
  518.8 8.5 %collective-permute-start.19 = (f32[2,4,130,1]{2,1,3,0:T(4,128)S(1)}, f32[2,4,130,1]{2,1,3,0:T(4,128)S(1)}, u32[]{:S(2)}, u32[]{:S(2)}) collective-permute-start(f32[2,4,130,1]{2,1,3,0:T(4,128)S(1)} %copy.108), channel_id=1, source_target_pairs={{1,0},{2,1},{3,2},{4,3},{5,4},{6,5},{7,6},{8,7},{9,8},{10,9},{11,1... | collective-permute-start | bytes 12488 | tf_op jit(solution)/shard_map/ppermute | solution.py:29
  523.9 4.5 collective-permute-start.18
  612.7 121.3 %copy-start.2 = (f32[2,4,128,128]{3,2,1,0:T(8,128)}, f32[2,4,128,128]{3,2,1,0:T(8,128)S(1)}, u32[]{:S(2)}) copy-start(f32[2,4,128,128]{3,2,1,0:T(8,128)S(1)} %get-tuple-element.16) | copy-start | bytes 1572868
  612.8 105.6 %collective-permute-start.21 = (f32[2,4,64,128]{3,2,1,0:T(8,128)S(1)}, f32[2,4,64,128]{3,2,1,0:T(8,128)S(1)}, u32[]{:S(2)}, u32[]{:S(2)}) collective-permute-start(f32[2,4,64,128]{3,2,1,0:T(8,128)S(1)} %get-tuple-element.37), channel_id=1, source_target_pairs={{16,0},{32,16},{48,32},{64,48},{80,64},{96,80},{112,96},{128,112},... | collective-permute-start | bytes 786440 | tf_op jit(solution)/shard_map/ppermute | solution.py:29
  614.1 104.4 %collective-permute-start.20 = (f32[2,4,64,128]{3,2,1,0:T(8,128)S(1)}, f32[2,4,64,128]{3,2,1,0:T(8,128)S(1)}, u32[]{:S(2)}, u32[]{:S(2)}) collective-permute-start(f32[2,4,64,128]{3,2,1,0:T(8,128)S(1)} %get-tuple-element.36), channel_id=1, source_target_pairs={{0,16},{16,32},{32,48},{48,64},{64,80},{80,96},{96,112},{112,128},... | collective-permute-start | bytes 786440 | tf_op jit(solution)/shard_map/ppermute | solution.py:27
  720.6 10.7 %collective-permute-start.23 = (f32[2,4,256,64]{2,3,1,0:T(8,128)}, f32[2,4,256,64]{2,3,1,0:T(8,128)S(1)}, u32[]{:S(2)}, u32[]{:S(2)}) collective-permute-start(f32[2,4,256,64]{2,3,1,0:T(8,128)} %copy.115), channel_id=1, source_target_pairs={{1,0},{2,1},{3,2},{4,3},{5,4},{6,5},{7,6},{8,7},{9,8},{10,9},{11,1... | collective-permute-start | bytes 1572872 | tf_op jit(solution)/shard_map/ppermute | solution.py:29
  723.0 9.6 %collective-permute-start.22 = (f32[2,4,256,64]{2,3,1,0:T(8,128)S(1)}, f32[2,4,256,64]{2,3,1,0:T(8,128)}, u32[]{:S(2)}, u32[]{:S(2)}) collective-permute-start(f32[2,4,256,64]{2,3,1,0:T(8,128)S(1)} %copy.114), channel_id=1, source_target_pairs={{0,1},{1,2},{2,3},{3,4},{4,5},{5,6},{6,7},{7,8},{8,9},{9,10},{10,1... | collective-permute-start | bytes 1572872 | tf_op jit(solution)/shard_map/ppermute | solution.py:27
  (29 other events, 162.7 us)
where the time goes:
time: 770 us; the launch traced here: 762 us
  blocking collectives  534 us (69%)
  matrix products  70.3 us (9%)
  starting transfers between devices  67.9 us (9%)
  local copies, waits for them, and re-layouts  58.5 us (8%)
  other arithmetic  24.1 us (3%)
    psum x2, blocking collectives, rz_sum(): return lax.psum(inner_local(left_arr, right_arr), ('rows', 'cols'))  153 us
    unnamed x3, blocking collectives  137 us
    psum x3, blocking collectives, precondition(): owned = lax.psum(owned, 'rows')  91.1 us
    psum x1, blocking collectives, shards(): alpha = rz_now / lax.psum(inner_local(direction, image), ('rows', 'cols'))  78.1 us
    all_gather x3, blocking collectives, precondition(): every_sol = lax.all_gather(own_sol, 'cols', axis=0, tiled=True)  74.4 us
    ppermute x12, starting transfers between devices, with_halo(): lax.ppermute(tail, axis, [(i, (i + 1) % count) for i in range(ends)])  46.4 us
    ppermute x12, starting transfers between devices, with_halo(): lax.ppermute(head, axis, [((i + 1) % count, i) for i in range(ends)])  21.5 us
    dot_general x6, matrix products, block_solve(): result = jnp.einsum('vtxiyb,bj->vtxiyj', result, basis, precision=HIGH)  20.4 us
  transfers between devices with their start and end apart: 24, of which 7 were waited for; matrix products, arithmetic and copies ran while one was open for 5% of the time, Pallas kernels for 0%

commit v1 on v0

v1 whole, which is shorter than its diff:
```python
import math

import numpy as np

import jax
import jax.numpy as jnp
from jax import lax
from jax.experimental import pallas as pl
from jax.experimental.pallas import tpu as pltpu
from jax.sharding import PartitionSpec as P

SUB = 128
HALF = 64
VARS = 2
TIERS = 4
SLABS = VARS * TIERS
SHIFT_C = 0.5
SINK_C = 0.05
HIGH = lax.Precision.HIGHEST
F32 = jnp.float32
BF16 = jnp.bfloat16
BOTH = ("rows", "cols")
EXT = 2 * SUB


def _split(mat):
    mat = np.asarray(mat, np.float32)
    top = mat.astype(BF16)
    low = (mat - top.astype(np.float32)).astype(BF16)
    return top, low


def _constants():
    n = np.arange(1, SUB + 1, dtype=np.float64)
    ang = math.pi / (SUB + 1)
    s = math.sqrt(2.0 / (SUB + 1)) * np.sin(ang * n[:, None] * n[None, :])
    ev = 2.0 - 2.0 * np.cos(ang * n)
    den = (ev[:, None] + ev[None, :] + SHIFT_C).astype(np.float32)
    pair = np.zeros((EXT, EXT))
    pair[:SUB, :SUB] = s
    pair[SUB:, SUB:] = s
    fwd = np.zeros((EXT, EXT))
    fwd[0:HALF, :SUB] = s[HALF:, :]
    fwd[SUB : SUB + HALF, :SUB] = s[:HALF, :]
    fwd[HALF:SUB, SUB:] = s[:HALF, :]
    fwd[SUB + HALF :, SUB:] = s[HALF:, :]
    inv = np.zeros((EXT, EXT))
    inv[:SUB, 0:HALF] = s[:, HALF:]
    inv[SUB:, HALF:SUB] = s[:, :HALF]
    inv_r = inv.copy()
    inv_r[:SUB, SUB] = s[:, HALF - 1]
    inv_r[SUB:, SUB + 1] = s[:, HALF]
    inv_c = inv.copy()
    inv_c[:SUB, SUB] = s[:, HALF - 1]
    inv_c[SUB:, EXT - 1] = s[:, HALF]
    return den, _split(pair), _split(fwd), _split(inv_r), _split(inv_c)


def _mm(x, top, low):
    xh = x.astype(BF16)
    xl = (x - xh.astype(F32)).astype(BF16)
    acc = jnp.dot(xh, top, preferred_element_type=F32)
    acc = acc + jnp.dot(xl, top, preferred_element_type=F32)
    return acc + jnp.dot(xh, low, preferred_element_type=F32)


def _iota(shape, dim):
    return lax.broadcasted_iota(jnp.int32, shape, dim)


def _tier_scalars(table, tiers):
    rows = []
    for t in range(TIERS):
        pick = tiers[t]
        rows.append([table[pick, m] for m in range(table.shape[1])])
    return rows


def _mean(row):
    total = row[0]
    for value in row[1:]:
        total = total + value
    return total * (1.0 / len(row))


def _flip2(x):
    return jnp.concatenate([x[:, :SUB].T, x[:, SUB:].T], axis=1)


def _aligned_tier(f0, f1, dinv, top, low):
    x = _mm(jnp.concatenate([f0, f1], axis=1), top, low)
    x = _mm(_flip2(x), top, low)
    x = x * jnp.concatenate([dinv, dinv], axis=1)
    x = _mm(x, top, low)
    x = _mm(_flip2(x), top, low)
    return x[:, :SUB], x[:, SUB:]


def _column_edges(get, count, col):
    lane = _iota((SUB, SUB), 1)
    acc = jnp.zeros((SUB, SUB), F32)
    for k in range(count):
        rolled = pltpu.roll(get(k), (k - col) % SUB, 1)
        acc = jnp.where(lane == k, rolled, acc)
    return acc.T[:16]


def _payload(values, ref):
    lane = _iota((1, SUB), 1)
    row = jnp.zeros((1, SUB), F32)
    for k, value in enumerate(values):
        row = jnp.where(lane == k, value, row)
    ref[...] = jnp.broadcast_to(row, ref.shape)


def _gathered(w_ref, gath_ref):
    return jnp.dot(w_ref[...], gath_ref[...], precision=HIGH, preferred_element_type=F32)


def _take(arr, row, lane):
    hit = (_iota(arr.shape, 0) == row) & (_iota(arr.shape, 1) == lane)
    return jnp.sum(jnp.where(hit, arr, 0.0))


def _ratio(arr, dist):
    return arr / pltpu.roll(arr, arr.shape[1] - dist, 1)


def _first(power, send_n, send_s, pay):
    sums = []
    for v in range(VARS):
        total = jnp.zeros((SUB, SUB), F32)
        for t in range(TIERS):
            x = power[v, t]
            send_n[v, t] = x[:HALF]
            send_s[v, t] = x[HALF:]
            total = total + x
        sums.append(jnp.sum(total))
    _payload(sums, pay)


def _prepare(n_rows, n_cols, own, power, material, table, tiers, slot_s, slot_v, inverse, den, top, low,
             al, cond, edge_n, edge_s, edge_w, edge_e, w_out):
    rows = _tier_scalars(table, tiers)
    for t in range(TIERS):
        mat = material[t]
        c = jnp.zeros((SUB, SUB), F32)
        for m, value in enumerate(rows[t]):
            c = jnp.where(mat == m, value, c)
        cond[t] = c
        dinv = 1.0 / (_mean(rows[t]) * den[...])
        a0, a1 = _aligned_tier(power[0, t], power[1, t], dinv, top[...], low[...])
        al[0, t] = a0
        al[1, t] = a1
    _edges(al, cond, edge_n, edge_s, edge_w, edge_e)
    total = n_rows * n_cols
    me = lax.axis_index("rows") * n_cols + lax.axis_index("cols")
    sub = _iota((8, total), 0)
    lane = _iota((8, total), 1)
    mine = jnp.full((8, total), -1, jnp.int32)
    for k, step in enumerate((0, -n_cols, n_cols, -1, 1)):
        g = jnp.minimum(jnp.maximum(me + step, 0), total - 1)
        mine = jnp.where(sub == k, slot_s[g], mine)
    picked = jnp.dot((mine == lane).astype(F32), inverse[...], precision=HIGH, preferred_element_type=F32)
    spread = (_iota((own, total), 1) % own == _iota((own, total), 0)).astype(F32)
    full = jnp.dot(picked, spread, precision=HIGH, preferred_element_type=F32)
    full = jnp.where((lane // own) == (mine // own), full, 0.0)
    place = (_iota((total, total), 0) == slot_v[...]).astype(F32)
    weights = jnp.dot(full, place, precision=HIGH, preferred_element_type=F32)
    weights = weights * (1.0 / (SUB * SUB * TIERS))
    w_out[...] = jnp.where(sub == 5, 1.0, weights)


def _edges(al, cond, edge_n, edge_s, edge_w, edge_e):
    for k in range(SLABS):
        edge_n[k : k + 1, :] = al[k // TIERS, k % TIERS, 0:1, :]
        edge_s[k : k + 1, :] = al[k // TIERS, k % TIERS, SUB - 1 : SUB, :]
    pad = jnp.zeros((16 - SLABS, SUB), F32)
    edge_n[SLABS:, :] = pad
    edge_s[SLABS:, :] = pad
    count = SLABS
    if cond is not None:
        count += TIERS
        for t in range(TIERS):
            edge_n[SLABS + t : SLABS + t + 1, :] = cond[t, 0:1, :]
            edge_s[SLABS + t : SLABS + t + 1, :] = cond[t, SUB - 1 : SUB, :]

    def get(k):
        return al[k // TIERS, k % TIERS] if k < SLABS else cond[k - SLABS]

    edge_w[...] = _column_edges(get, count, 0)
    edge_e[...] = _column_edges(get, count, SUB - 1)


def _align(with_edges, f, table, tiers, den, top, low, al, *edges):
    rows = _tier_scalars(table, tiers)
    for t in range(TIERS):
        dinv = 1.0 / (_mean(rows[t]) * den[...])
        a0, a1 = _aligned_tier(f[0, t], f[1, t], dinv, top[...], low[...])
        al[0, t] = a0
        al[1, t] = a1
    if with_edges:
        _edges(al, None, *edges)


def _pack(with_edges, f, got_n, got_s, *rest):
    if with_edges:
        edge_w, edge_e, send_w, send_e = rest
        send_w[TIERS * EXT :, :] = edge_w[...]
        send_e[TIERS * EXT :, :] = edge_e[...]
    else:
        send_w, send_e = rest
    for t in range(TIERS):
        at = t * EXT
        for part, size, start in ((f, SUB, 0), (got_n, HALF, SUB), (got_s, HALF, SUB + HALF)):
            x0 = part[0, t]
            x1 = part[1, t]
            left = _iota((size, SUB), 1) < HALF
            send_w[at + start : at + start + size, :] = jnp.where(left, x0, pltpu.roll(x1, HALF, 1))
            send_e[at + start : at + start + size, :] = jnp.where(left, pltpu.roll(x0, HALF, 1), x1)


def _offset_tier(t, halo, f, got_n, got_s, got_w, got_e, scale, fwd, inv_r, inv_c):
    wm = got_w[t * EXT : (t + 1) * EXT, :]
    em = got_e[t * EXT : (t + 1) * EXT, :]
    left = _iota((EXT, SUB), 1) < HALF
    side = (jnp.where(left, wm, pltpu.roll(em, HALF, 1)), jnp.where(left, pltpu.roll(wm, HALF, 1), em))
    stack = []
    for v in range(VARS):
        mid = jnp.concatenate([f[v, t], got_n[v, t], got_s[v, t]], axis=0)
        stack.append(jnp.concatenate([mid, side[v]], axis=1))
    x = _mm(jnp.concatenate(stack, axis=0), *fwd)
    x = jnp.concatenate([x[:EXT].T, x[EXT:].T], axis=0)
    x = _mm(x, *fwd)
    x = x * jnp.concatenate([scale, scale], axis=0)
    if halo:
        x = _mm(x, *inv_r)
        tall = [x[:EXT, :SUB].T, x[EXT:, :SUB].T, x[:EXT, SUB:].T[:8], x[EXT:, SUB:].T[:8]]
    else:
        x = _mm(x, inv_r[0][:, :SUB], inv_r[1][:, :SUB])
        tall = [x[:EXT].T, x[EXT:].T]
    x = jnp.concatenate(tall, axis=0)
    if not halo:
        x = _mm(x, inv_c[0][:, :SUB], inv_c[1][:, :SUB])
        return (x[:SUB], x[SUB:]), None, None
    x = _mm(x, *inv_c)
    tiles = (x[:SUB, :SUB], x[SUB:EXT, :SUB])
    sides = (x[:SUB, SUB:], x[SUB:EXT, SUB:])
    ends = (x[EXT : EXT + 8, :SUB], x[EXT + 8 :, :SUB])
    return tiles, ends, sides


def _scale(dinv):
    has_w = jnp.where(lax.axis_index("cols") > 0, 1.0, 0.0)
    has_n = jnp.where(lax.axis_index("rows") > 0, 1.0, 0.0)
    above = dinv * has_n
    return jnp.concatenate(
        [
            jnp.concatenate([above * has_w, dinv * has_w], axis=1),
            jnp.concatenate([above, dinv], axis=1),
        ],
        axis=0,
    )


def _solve(halo, f, got_n, got_s, got_w, got_e, al, near_n, near_s, table, tiers, den, fwd, inv_r, inv_c,
           y, y_rows, y_cols):
    rows = _tier_scalars(table, tiers)
    if halo:
        cols = _side_columns(got_w, got_e)
    for t in range(TIERS):
        dinv = 1.0 / (_mean(rows[t]) * den[...])
        tiles, ends, sides = _offset_tier(t, halo, f, got_n, got_s, got_w, got_e, _scale(dinv), fwd, inv_r, inv_c)
        for v in range(VARS):
            y[v, t] = tiles[v] + al[v, t]
            if halo:
                k = v * TIERS + t
                sub = _iota((8, SUB), 0)
                near = jnp.where(sub == 0, near_n[k : k + 1, :], near_s[k : k + 1, :])
                y_rows[v, t] = ends[v] + near
                y_cols[v, t] = sides[v] + _column_pair(cols, k)


def _side_columns(got_w, got_e):
    base = TIERS * EXT
    pad = jnp.zeros((SUB - 32, SUB), F32)
    return jnp.concatenate([got_w[base:, :], got_e[base:, :], pad], axis=0).T


def _column_pair(cols, k):
    lane = _iota((SUB, SUB), 1)
    west = pltpu.roll(cols, (SUB - k) % SUB, 1)
    east = pltpu.roll(cols, (SUB - 1 - 16 - k) % SUB, 1)
    return jnp.where(lane < HALF, west, east)


def _shifts(x, row_n, row_s, side):
    sub = _iota((SUB, SUB), 0)
    lane = _iota((SUB, SUB), 1)
    north = jnp.where(sub == 0, row_n, pltpu.roll(x, 1, 0))
    south = jnp.where(sub == SUB - 1, row_s, pltpu.roll(x, SUB - 1, 0))
    west = jnp.where(lane == 0, side, pltpu.roll(x, 1, 1))
    east = jnp.where(lane == SUB - 1, side, pltpu.roll(x, SUB - 1, 1))
    return north, south, west, east


def _inside(n_rows, n_cols):
    r = lax.axis_index("rows")
    c = lax.axis_index("cols")
    one = jnp.float32(1.0)
    zero = jnp.float32(0.0)
    return (
        jnp.where(r > 0, one, zero),
        jnp.where(r < n_rows - 1, one, zero),
        jnp.where(c > 0, one, zero),
        jnp.where(c < n_cols - 1, one, zero),
    )


def _operate(z, z_rows, z_cols, cond, c_rows, c_cols, out):
    for t in range(TIERS):
        c = cond[t]
        near = _shifts(c, c_rows[t, 0:1, :], c_rows[t, 1:2, :], c_cols[t])
        coefs = [0.5 * (c + n) for n in near]
        for v in range(VARS):
            u = z[v, t]
            around = _shifts(u, z_rows[v, t, 0:1, :], z_rows[v, t, 1:2, :], z_cols[v, t])
            acc = coefs[0] * (u - around[0])
            for k in range(1, 4):
                acc = acc + coefs[k] * (u - around[k])
            if t + 1 < TIERS:
                acc = acc + (c + cond[t + 1]) * (u - z[v, t + 1])
            if t > 0:
                acc = acc - (cond[t - 1] + c) * (z[v, t - 1] - u)
            if t == 0:
                acc = acc + SINK_C * c * u
            out[v, t] = acc


def _dot(a, b, v):
    total = jnp.zeros((SUB, SUB), F32)
    for t in range(TIERS):
        total = total + (a[v, t] * b[v, t] if b is not None else a[v, t])
    return jnp.sum(total)


def _begin(n_rows, n_cols, power, got_n, got_s, got_w, got_e, al, near_n, near_s, cond, w_ref, gath, table, tiers,
           den, fh, fl, rh, rl, ch, cl,
           y, y_rows, y_cols, s, send_n, send_s, pay, c_rows, c_cols, e_out, z, z_rows, z_cols):
    _solve(True, power, got_n, got_s, got_w, got_e, al, near_n, near_s, table, tiers, den,
           (fh[...], fl[...]), (rh[...], rl[...]), (ch[...], cl[...]), y, y_rows, y_cols)
    cols = _side_columns(got_w, got_e)
    sub = _iota((8, SUB), 0)
    for t in range(TIERS):
        k = SLABS + t
        c_rows[t] = jnp.where(sub == 0, near_n[k : k + 1, :], near_s[k : k + 1, :])
        c_cols[t] = _column_pair(cols, k)
    e = _gathered(w_ref, gath)
    e_out[...] = e
    inside = _inside(n_rows, n_cols)
    _add_coarse(e, 0, inside, y, y_rows, y_cols, z, z_rows, z_cols)
    _operate(z, z_rows, z_cols, cond, c_rows, c_cols, s)
    _send_rows(s, send_n, send_s)
    _payload(
        [_dot(power, z, v) for v in range(VARS)]
        + [_dot(z, s, v) for v in range(VARS)]
        + [_dot(s, None, v) for v in range(VARS)],
        pay,
    )


def _send_rows(s, send_n, send_s):
    for v in range(VARS):
        for t in range(TIERS):
            send_n[v, t] = s[v, t, :HALF]
            send_s[v, t] = s[v, t, HALF:]


def _add_coarse(e, base, inside, y, y_rows, y_cols, z, z_rows, z_cols):
    sub = _iota((8, SUB), 0)
    lane = _iota((SUB, SUB), 1)
    for v in range(VARS):
        own, north, south, west, east = [_take(e, k, base + v) for k in range(5)]
        for t in range(TIERS):
            z[v, t] = y[v, t] + own
            z_rows[v, t] = jnp.where(sub == 0, (y_rows[v, t] + north) * inside[0], (y_rows[v, t] + south) * inside[1])
            z_cols[v, t] = jnp.where(
                lane < HALF, (y_cols[v, t] + west) * inside[2], (y_cols[v, t] + east) * inside[3]
            )


def _second(f, got_n, got_s, got_w, got_e, al, near_n, near_s, table, tiers, den, fh, fl, rh, rl, ch, cl,
            y, y_rows, y_cols):
    _solve(True, f, got_n, got_s, got_w, got_e, al, near_n, near_s, table, tiers, den,
           (fh[...], fl[...]), (rh[...], rl[...]), (ch[...], cl[...]), y, y_rows, y_cols)


def _step(n_rows, n_cols, power, s0, y0, y0_rows, y0_cols, y1, y1_rows, y1_cols, cond, c_rows, c_cols, w_ref, e0,
          gath, r1, z1, w1, send_n, send_s, pay, keep, z_rows, z_cols):
    res = _gathered(w_ref, gath)
    quotient = _ratio(res, 2)
    alphas = [_take(quotient, 5, v) for v in range(VARS)]
    lane = _iota(res.shape, 1)
    moved = pltpu.roll(res, res.shape[1] - 4, 1)
    alpha_row = jnp.where(lane == 0, alphas[0], alphas[1])
    e1 = e0[...] - alpha_row * moved
    inside = _inside(n_rows, n_cols)
    sub = _iota((8, SUB), 0)
    wide = _iota((SUB, SUB), 1)
    for v in range(VARS):
        own, north, south, west, east = [_take(e1, k, v) for k in range(5)]
        a = alphas[v]
        for t in range(TIERS):
            r1[v, t] = power[v, t] - a * s0[v, t]
            z1[v, t] = (y0[v, t] - a * y1[v, t]) + own
            ends = y0_rows[v, t] - a * y1_rows[v, t]
            z_rows[v, t] = jnp.where(sub == 0, (ends + north) * inside[0], (ends + south) * inside[1])
            side = y0_cols[v, t] - a * y1_cols[v, t]
            z_cols[v, t] = jnp.where(wide < HALF, (side + west) * inside[2], (side + east) * inside[3])
    _operate(z1, z_rows, z_cols, cond, c_rows, c_cols, w1)
    _send_rows(w1, send_n, send_s)
    _payload(
        [_dot(r1, z1, v) for v in range(VARS)]
        + [_dot(z1, w1, v) for v in range(VARS)]
        + [_dot(z1, s0, v) for v in range(VARS)]
        + [_dot(w1, None, v) for v in range(VARS)],
        pay,
    )
    row = jnp.zeros((8, SUB), F32)
    kl = _iota((8, SUB), 1)
    for v in range(VARS):
        for k, value in enumerate(
            (_take(res, 5, v), _take(res, 5, 2 + v), alphas[v], _take(e0[...], 0, v), _take(res, 0, 4 + v))
        ):
            row = jnp.where(kl == 2 * k + v, value, row)
    keep[...] = row


def _third(f, got_n, got_s, got_w, got_e, al, table, tiers, den, fh, fl, rh, rl, ch, cl, y):
    _solve(False, f, got_n, got_s, got_w, got_e, al, None, None, table, tiers, den,
           (fh[...], fl[...]), (rh[...], rl[...]), (ch[...], cl[...]), y, None, None)


def _finish(s0, y0, y1, r1, z1, w1, y2, w_ref, keep, gath, x_out, r_out, z_out):
    res = _gathered(w_ref, gath)
    k = keep[...]
    for v in range(VARS):
        def wide(value):
            return jnp.full((8, SUB), 1.0, F32) * value

        rz0, d0, a0, e0, cs = [_take(k, 0, 2 * j + v) for j in range(5)]
        rz1, d1, zs = [_take(res, 5, 2 * j + v) for j in range(3)]
        cw = _take(res, 0, 6 + v)
        beta_w = wide(rz1) / wide(rz0)
        den = wide(d1) + 2.0 * beta_w * wide(zs) + beta_w * beta_w * wide(d0)
        alpha = _take(wide(rz1) / den, 0, 0)
        beta = _take(beta_w, 0, 0)
        change = -alpha * (cw + beta * cs)
        for t in range(TIERS):
            z = z1[v, t]
            x_out[v, t] = a0 * (y0[v, t] + e0) + alpha * (z + beta * (y0[v, t] + e0))
            r_out[v, t] = r1[v, t] - alpha * (w1[v, t] + beta * s0[v, t])
            z_out[v, t] = (z - alpha * (y2[v, t] + beta * y1[v, t])) + change


def _call(body, outs, args, smem=(), scratch=()):
    specs = [
        pl.BlockSpec(memory_space=pltpu.SMEM if i in smem else pltpu.VMEM) for i in range(len(args))
    ]
    return pl.pallas_call(
        body,
        out_shape=[jax.ShapeDtypeStruct(s, F32) for s in outs],
        in_specs=specs,
        out_specs=[pl.BlockSpec(memory_space=pltpu.VMEM) for _ in outs],
        scratch_shapes=[pltpu.VMEM(s, F32) for s in scratch],
        compiler_params=pltpu.CompilerParams(vmem_limit_bytes=48 << 20),
    )(*args)


FIELD = (VARS, TIERS, SUB, SUB)
MARGIN = (VARS, TIERS, HALF, SUB)
ENDS = (VARS, TIERS, 8, SUB)
EDGE = (16, SUB)


def _exchange(first, second, axis):
    count = lax.axis_size(axis)
    before = lax.ppermute(second, axis, [(i, i + 1) for i in range(count - 1)])
    after = lax.ppermute(first, axis, [(i + 1, i) for i in range(count - 1)])
    return before, after


def _everywhere(pay):
    return lax.all_to_all(pay, BOTH, 0, 0, tiled=True)


def shards(power, material, cond_table, tier_table, coarse_slot, coarse_inverse):
    n_rows = lax.axis_size("rows")
    n_cols = lax.axis_size("cols")
    total = n_rows * n_cols
    own = coarse_inverse.shape[1]
    den, pair, fwd, inv_r, inv_c = _constants()
    den = jnp.asarray(den)
    pair, fwd, inv_r, inv_c = [tuple(jnp.asarray(m) for m in two) for two in (pair, fwd, inv_r, inv_c)]
    mats = (den, *fwd, *inv_r, *inv_c)
    pay_shape = (total, SUB)
    message = (TIERS * EXT + 16, SUB)
    bare = (TIERS * EXT, SUB)

    send_n, send_s, pay = _call(_first, [MARGIN, MARGIN, pay_shape], [power])
    gath_a = _everywhere(pay)
    got_n, got_s = _exchange(send_n, send_s, "rows")
    al, cond, edge_n, edge_s, edge_w, edge_e, weights = _call(
        lambda *refs: _prepare(n_rows, n_cols, own, *refs),
        [FIELD, (TIERS, SUB, SUB), EDGE, EDGE, EDGE, EDGE, (8, total)],
        [power, material, cond_table, tier_table, coarse_slot, coarse_slot.reshape(1, total),
         coarse_inverse.reshape(total, own), den, *pair],
        smem=(2, 3, 4),
    )
    near_n, near_s = _exchange(edge_n, edge_s, "rows")
    send_w, send_e = _call(
        lambda *refs: _pack(True, *refs), [message, message], [power, got_n, got_s, edge_w, edge_e]
    )
    got_w, got_e = _exchange(send_w, send_e, "cols")
    y0, y0_rows, y0_cols, s0, send_n, send_s, pay, c_rows, c_cols, e0 = _call(
        lambda *refs: _begin(n_rows, n_cols, *refs),
        [FIELD, ENDS, FIELD, FIELD, MARGIN, MARGIN, pay_shape, (TIERS, 8, SUB), (TIERS, SUB, SUB), (8, SUB)],
        [power, got_n, got_s, got_w, got_e, al, near_n, near_s, cond, weights, gath_a, cond_table, tier_table, *mats],
        smem=(11, 12),
        scratch=(FIELD, ENDS, FIELD),
    )

    gath_b = _everywhere(pay)
    got_n, got_s = _exchange(send_n, send_s, "rows")
    al, edge_n, edge_s, edge_w, edge_e = _call(
        lambda *refs: _align(True, *refs),
        [FIELD, EDGE, EDGE, EDGE, EDGE],
        [s0, cond_table, tier_table, den, *pair],
        smem=(1, 2),
    )
    near_n, near_s = _exchange(edge_n, edge_s, "rows")
    send_w, send_e = _call(
        lambda *refs: _pack(True, *refs), [message, message], [s0, got_n, got_s, edge_w, edge_e]
    )
    got_w, got_e = _exchange(send_w, send_e, "cols")
    y1, y1_rows, y1_cols = _call(
        _second,
        [FIELD, ENDS, FIELD],
        [s0, got_n, got_s, got_w, got_e, al, near_n, near_s, cond_table, tier_table, *mats],
        smem=(8, 9),
    )
    r1, z1, w1, send_n, send_s, pay, keep = _call(
        lambda *refs: _step(n_rows, n_cols, *refs),
        [FIELD, FIELD, FIELD, MARGIN, MARGIN, pay_shape, (8, SUB)],
        [power, s0, y0, y0_rows, y0_cols, y1, y1_rows, y1_cols, cond, c_rows, c_cols, weights, e0, gath_b],
        scratch=(ENDS, FIELD),
    )

    gath_c = _everywhere(pay)
    got_n, got_s = _exchange(send_n, send_s, "rows")
    (al,) = _call(
        lambda *refs: _align(False, *refs), [FIELD], [w1, cond_table, tier_table, den, *pair], smem=(1, 2)
    )
    send_w, send_e = _call(lambda *refs: _pack(False, *refs), [bare, bare], [w1, got_n, got_s])
    got_w, got_e = _exchange(send_w, send_e, "cols")
    (y2,) = _call(
        _third, [FIELD], [w1, got_n, got_s, got_w, got_e, al, cond_table, tier_table, *mats], smem=(6, 7)
    )
    return tuple(
        _call(_finish, [FIELD, FIELD, FIELD], [s0, y0, y1, r1, z1, w1, y2, weights, keep, gath_c])
    )


def solution(mesh):
    in_specs = (P(None, None, "rows", "cols"), P(None, "rows", "cols"), P(), P(), P(), P())
    out_specs = (P(None, None, "rows", "cols"),) * 3
    return jax.shard_map(shards, mesh=mesh, in_specs=in_specs, out_specs=out_specs, check_vma=False)
```

time: 770 us -> 185 us (0.24)
  blocking collectives: 534 us -> 0 us
  matrix products: 70.3 us -> 0 us
  Pallas kernels: 0 us -> 45.3 us
  local copies, waits for them, and re-layouts: 58.5 us -> 19.7 us
  starting transfers between devices: 67.9 us -> 93 us
  other arithmetic: 24.1 us -> 0 us
  waiting for transfers between devices: 6.15 us -> 24.3 us
    psum x6 -> x0, blocking collectives: 322 us -> none  [the longest x2 153 us: rz_sum(): return lax.psum(inner_local(left_arr, right_arr), ('rows', 'cols'))]
    unnamed x3 -> x0, blocking collectives: 137 us -> none
    all_gather x3 -> x0, blocking collectives: 74.4 us -> none  [precondition(): every_sol = lax.all_gather(own_sol, 'cols', axis=0, tiled=True)]
    dot_general x31 -> x0, matrix products: 70.3 us -> none  [the longest x6 20.4 us: block_solve(): result = jnp.einsum('vtxiyb,bj->vtxiyj', result, basis, precision=HIGH)]
    all_to_all x0 -> x3, starting transfers between devices: none -> 49.4 us  [_everywhere(): return lax.all_to_all(pay, BOTH, 0, 0, tiled=True)]
    pallas_call x0 -> x12, Pallas kernels: none -> 45.3 us  [_call(): pl.pallas_call(body, out_shape=[jax.ShapeDtypeStruct(s, F32) for s in out...]
    ppermute x24 -> x16, starting transfers between devices: 67.9 us -> 43.6 us  [the longest x8 31.2 us: _exchange(): before = lax.ppermute(second, axis, [(i, i + 1) for i in range(count - 1)])]
    reshape x6 -> x0, local copies, waits for them, and re-layouts: 17.6 us -> none  [the longest x3 9.29 us: block_solve(): return result.reshape(shape)]
  transfers between devices with their start and end apart: 24 -> 19, of which waited for: 7 -> 7; matrix products, arithmetic and copies ran while one was open for 5% -> 0% of each run, Pallas kernels for 0% -> 14%
where the time goes in v1:
time: 185 us; the launch traced here: 183 us
  starting transfers between devices  93 us (50%)
  Pallas kernels  45.3 us (24%)
  waiting for transfers between devices  24.3 us (13%)
  local copies, waits for them, and re-layouts  19.7 us (11%)
    all_to_all x3, starting transfers between devices, _everywhere(): return lax.all_to_all(pay, BOTH, 0, 0, tiled=True)  49.4 us
    pallas_call x12, Pallas kernels, _call(): pl.pallas_call(body, out_shape=[jax.ShapeDtypeStruct(s, F32) for s in out...  45.3 us
    ppermute x8, starting transfers between devices, _exchange(): before = lax.ppermute(second, axis, [(i, i + 1) for i in range(count - 1)])  31.2 us
    unnamed x104, local copies, waits for them, and re-layouts  19.7 us
    ppermute x8, waiting for transfers between devices, _exchange(): after = lax.ppermute(first, axis, [(i + 1, i) for i in range(count - 1)])  16.4 us
    ppermute x8, starting transfers between devices, _exchange(): after = lax.ppermute(first, axis, [(i + 1, i) for i in range(count - 1)])  12.4 us
    all_to_all x3, waiting for transfers between devices, _everywhere(): return lax.all_to_all(pay, BOTH, 0, 0, tiled=True)  4.88 us
  transfers between devices with their start and end apart: 19, of which 7 were waited for; matrix products, arithmetic and copies ran while one was open for 0% of the time, Pallas kernels for 14%

profile of v1, /device:TPU:1, one launch (start us, length us, event | category | flops | bytes accessed | tf_op | source)
XLA Modules:
  0.0 183.4 jit_solution(15492448454503311512)
XLA Ops:
  0.6 1.0 copy-done
  2.5 4.0 %collective-permute-start = (f32[2,4,64,128]{3,2,1,0:T(8,128)S(1)}, f32[2,4,64,128]{3,2,1,0:T(8,128)S(1)}, u32[]{:S(2)}, u32[]{:S(2)}) collective-permute-start(f32[2,4,64,128]{3,2,1,0:T(8,128)S(1)} %get-tuple-element.44), channel_id=1, source_target_pairs={{0,16},{16,32},{32,48},{48,64},{64,80},{80,96},{96,112},{112,128},... | collective-permute-start | bytes 786440 | tf_op jit(solution)/shard_map/ppermute | solution.py:488
  6.6 1.3 collective-permute-start.1
  8.6 0.9 copy-done.39
  9.5 3.7 %shard_map.167 = (f32[2,4,128,128]{3,2,1,0:T(8,128)S(1)}, f32[4,128,128]{2,1,0:T(8,128)S(1)}, f32[16,128]{1,0:T(8,128)S(1)}, f32[16,128]{1,0:T(8,128)S(1)}, f32[...) custom-call(f32[2,4,128,128]{3,2,1,0:T(8,128)S(1)} %copy-done, s32[4,128,128]{2,1,0:T(8,128)S(1)} %copy-done.39, ...), custom_call_target="tpu_custom_call" | custom-call | tf_op jit(solution)/shard_map/pallas_call | solution.py:470
  13.2 2.1 %collective-permute-done.1.refs_2_ = f32[2,4,64,128]{3,2,1,0:T(8,128)S(1)} collective-permute-done((f32[2,4,64,128]{3,2,1,0:T(8,128)S(1)}, f32[2,4,64,128]{3,2,1,0:T(8,128)S(1)}, u32[]{:S(2)}, u32[]{:S(2)}) %collective-permute-start.1) | collective-permute-done | bytes 262176 | tf_op jit(solution)/shard_map/ppermute | solution.py:489
  15.4 1.3 shard_map.168
  16.7 5.2 %collective-permute-start.2 = (f32[1040,128]{1,0:T(8,128)}, f32[1040,128]{1,0:T(8,128)}, u32[]{:S(2)}, u32[]{:S(2)}) collective-permute-start(f32[1040,128]{1,0:T(8,128)} %get-tuple-element.48), channel_id=1, source_target_pairs={{0,1},{1,2},{2,3},{3,4},{4,5},{5,6},{6,7},{7,8},{8,9},{9,10},{10,1... | collective-permute-start | bytes 1597448 | tf_op jit(solution)/shard_map/ppermute | solution.py:488
  22.0 1.9 %collective-permute-start.3 = (f32[1040,128]{1,0:T(8,128)}, f32[1040,128]{1,0:T(8,128)}, u32[]{:S(2)}, u32[]{:S(2)}) collective-permute-start(f32[1040,128]{1,0:T(8,128)} %get-tuple-element.49), channel_id=1, source_target_pairs={{1,0},{2,1},{3,2},{4,3},{5,4},{6,5},{7,6},{8,7},{9,8},{10,9},{11,1... | collective-permute-start | bytes 1597448 | tf_op jit(solution)/shard_map/ppermute | solution.py:489
  23.9 16.8 %all-to-all-start = ((f32[256,1,128]{2,1,0:T(1,128)}), f32[256,1,128]{2,1,0:T(1,128)S(1)}, u32[]{:S(2)}, u32[]{:S(2)}) async-start(f32[256,1,128]{2,1,0:T(1,128)} %bitcast.3), calls=%async_computation | async-start | bytes 262144 | tf_op jit(solution)/shard_map/all_to_all | solution.py:494
  40.7 3.3 %collective-permute-start.4 = (f32[16,128]{1,0:T(8,128)S(1)}, f32[16,128]{1,0:T(8,128)S(1)}, u32[]{:S(2)}, u32[]{:S(2)}) collective-permute-start(f32[16,128]{1,0:T(8,128)S(1)} %get-tuple-element.51), channel_id=1, source_target_pairs={{0,16},{16,32},{32,48},{48,64},{64,80},{80,96},{96,112},{112,128},... | collective-permute-start | bytes 24584 | tf_op jit(solution)/shard_map/ppermute | solution.py:488
  44.0 1.3 collective-permute-start.5
  45.3 3.4 %collective-permute-done.5.refs_7_ = f32[16,128]{1,0:T(8,128)S(1)} collective-permute-done((f32[16,128]{1,0:T(8,128)S(1)}, f32[16,128]{1,0:T(8,128)S(1)}, u32[]{:S(2)}, u32[]{:S(2)}) %collective-permute-start.5) | collective-permute-done | bytes 8224 | tf_op jit(solution)/shard_map/ppermute | solution.py:489
  48.7 4.9 %all-to-all-done = f32[256,1,128]{2,1,0:T(1,128)S(1)} async-done(((f32[256,1,128]{2,1,0:T(1,128)}), f32[256,1,128]{2,1,0:T(1,128)S(1)}, u32[]{:S(2)}, u32[]{:S(2)}) %all-to-all-start) | async-done | bytes 131104 | tf_op jit(solution)/shard_map/all_to_all | solution.py:494
  54.3 1.0 copy-done.32
  56.2 9.2 %shard_map.169 = (f32[2,4,128,128]{3,2,1,0:T(8,128)S(1)}, f32[2,4,8,128]{3,2,1,0:T(8,128)S(1)}, f32[2,4,128,128]{3,2,1,0:T(8,128)S(1)}, f32[2,4,128,128]{3,2,1,0...) custom-call(f32[2,4,128,128]{3,2,1,0:T(8,128)S(1)} %copy-done.1, ...), custom_call_target="tpu_custom_call" | custom-call | tf_op jit(solution)/shard_map/pallas_call | solution.py:470
  66.2 2.1 %collective-permute-start.6 = (f32[2,4,64,128]{3,2,1,0:T(8,128)S(1)}, f32[2,4,64,128]{3,2,1,0:T(8,128)S(1)}, u32[]{:S(2)}, u32[]{:S(2)}) collective-permute-start(f32[2,4,64,128]{3,2,1,0:T(8,128)S(1)} %get-tuple-element.58), channel_id=1, source_target_pairs={{0,16},{16,32},{32,48},{48,64},{64,80},{80,96},{96,112},{112,128},... | collective-permute-start | bytes 786440 | tf_op jit(solution)/shard_map/ppermute | solution.py:488
  68.3 1.5 collective-permute-start.7
  69.8 3.3 %shard_map.170 = (f32[2,4,128,128]{3,2,1,0:T(8,128)S(1)}, f32[16,128]{1,0:T(8,128)S(1)}, f32[16,128]{1,0:T(8,128)S(1)}, f32[16,128]{1,0:T(8,128)S(1)}, f32[16,128]{1,0:T(8,128)S(1)}) custom-call(f32[2,4,128,128]{3,2,1,0:T(8,128)S(1)} %get-tuple-element.56.refs_0_.f.refs_1_.s0, f32[4,8]{1,0:T(4,128)S(1)} %copy-done.43, s32[4]{0:T(128)S(1)} %copy-done.44, ...), custom_call_target="tpu_custom_call" | custom-call | tf_op jit(solution)/shard_map/pallas_call | solution.py:470
  73.2 3.5 %collective-permute-done.7.refs_2_.got_s = f32[2,4,64,128]{3,2,1,0:T(8,128)S(1)} collective-permute-done((f32[2,4,64,128]{3,2,1,0:T(8,128)S(1)}, f32[2,4,64,128]{3,2,1,0:T(8,128)S(1)}, u32[]{:S(2)}, u32[]{:S(2)}) %collective-permute-start.7) | collective-permute-done | bytes 262176 | tf_op jit(solution)/shard_map/ppermute | solution.py:489
  76.7 1.3 shard_map.171
  78.1 4.5 %collective-permute-start.8 = (f32[1040,128]{1,0:T(8,128)}, f32[1040,128]{1,0:T(8,128)}, u32[]{:S(2)}, u32[]{:S(2)}) collective-permute-start(f32[1040,128]{1,0:T(8,128)} %get-tuple-element.62), channel_id=1, source_target_pairs={{0,1},{1,2},{2,3},{3,4},{4,5},{5,6},{6,7},{7,8},{8,9},{9,10},{10,1... | collective-permute-start | bytes 1597448 | tf_op jit(solution)/shard_map/ppermute | solution.py:488
  82.6 1.9 %collective-permute-start.9 = (f32[1040,128]{1,0:T(8,128)}, f32[1040,128]{1,0:T(8,128)}, u32[]{:S(2)}, u32[]{:S(2)}) collective-permute-start(f32[1040,128]{1,0:T(8,128)} %get-tuple-element.63), channel_id=1, source_target_pairs={{1,0},{2,1},{3,2},{4,3},{5,4},{6,5},{7,6},{8,7},{9,8},{10,9},{11,1... | collective-permute-start | bytes 1597448 | tf_op jit(solution)/shard_map/ppermute | solution.py:489
  84.5 14.9 %all-to-all-start.1 = ((f32[256,1,128]{2,1,0:T(1,128)}), f32[256,1,128]{2,1,0:T(1,128)}, u32[]{:S(2)}, u32[]{:S(2)}) async-start(f32[256,1,128]{2,1,0:T(1,128)} %bitcast.16), calls=%async_computation.1 | async-start | bytes 262144 | tf_op jit(solution)/shard_map/all_to_all | solution.py:494
  99.4 3.3 %collective-permute-start.10 = (f32[16,128]{1,0:T(8,128)S(1)}, f32[16,128]{1,0:T(8,128)S(1)}, u32[]{:S(2)}, u32[]{:S(2)}) collective-permute-start(f32[16,128]{1,0:T(8,128)S(1)} %get-tuple-element.65), channel_id=1, source_target_pairs={{0,16},{16,32},{32,48},{48,64},{64,80},{80,96},{96,112},{112,128},... | collective-permute-start | bytes 24584 | tf_op jit(solution)/shard_map/ppermute | solution.py:488
  102.7 1.3 collective-permute-start.11
  104.0 3.5 %collective-permute-done.11.near_s = f32[16,128]{1,0:T(8,128)S(1)} collective-permute-done((f32[16,128]{1,0:T(8,128)S(1)}, f32[16,128]{1,0:T(8,128)S(1)}, u32[]{:S(2)}, u32[]{:S(2)}) %collective-permute-start.11) | collective-permute-done | bytes 8224 | tf_op jit(solution)/shard_map/ppermute | solution.py:489
  107.5 0.9 copy-done.14
  108.4 1.0 copy-done.30
  109.5 8.1 %shard_map.172 = (f32[2,4,128,128]{3,2,1,0:T(8,128)S(1)}, f32[2,4,8,128]{3,2,1,0:T(8,128)S(1)}, f32[2,4,128,128]{3,2,1,0:T(8,128)S(1)}) custom-call(f32[2,4,128,128]{3,2,1,0:T(8,128)S(1)} %get-tuple-element.56.refs_0_.f.refs_1_.s0, f32[2,4,64,128]{3,2,1,0:T(8,128)S(1)} %collective-permute-done.6.refs_1_.got_n, f32[2,4,64,128]{3,2,1,0:T(8,128)S(1)} %copy-done.14, ...), custom_call_target="tpu_custom_call" | custom-call | tf_op jit(solution)/shard_map/pallas_call | solution.py:470
  119.1 0.9 copy-done.16
  120.0 1.0 copy-done.22
  121.1 1.0 copy-done.24
  123.7 2.5 %shard_map.173 = (f32[2,4,128,128]{3,2,1,0:T(8,128)S(1)}, f32[2,4,128,128]{3,2,1,0:T(8,128)S(1)}, f32[2,4,128,128]{3,2,1,0:T(8,128)S(1)}, f32[2,4,64,128]{3,2,1,...) custom-call(f32[2,4,128,128]{3,2,1,0:T(8,128)S(1)} %copy-done.1, ...), custom_call_target="tpu_custom_call" | custom-call | tf_op jit(solution)/shard_map/pallas_call | solution.py:470
  127.1 3.1 %collective-permute-start.12 = (f32[2,4,64,128]{3,2,1,0:T(8,128)S(1)}, f32[2,4,64,128]{3,2,1,0:T(8,128)S(1)}, u32[]{:S(2)}, u32[]{:S(2)}) collective-permute-start(f32[2,4,64,128]{3,2,1,0:T(8,128)S(1)} %get-tuple-element.79), channel_id=1, source_target_pairs={{0,16},{16,32},{32,48},{48,64},{64,80},{80,96},{96,112},{112,128},... | collective-permute-start | bytes 786440 | tf_op jit(solution)/shard_map/ppermute | solution.py:488
  130.2 1.3 collective-permute-start.13
  131.5 2.9 %collective-permute-done.12.refs_1_.got_n = f32[2,4,64,128]{3,2,1,0:T(8,128)S(1)} collective-permute-done((f32[2,4,64,128]{3,2,1,0:T(8,128)S(1)}, f32[2,4,64,128]{3,2,1,0:T(8,128)S(1)}, u32[]{:S(2)}, u32[]{:S(2)}) %collective-permute-start.12) | collective-permute-done | bytes 262176 | tf_op jit(solution)/shard_map/ppermute | solution.py:488
  134.4 3.8 %collective-permute-done.13.refs_2_.got_s = f32[2,4,64,128]{3,2,1,0:T(8,128)S(1)} collective-permute-done((f32[2,4,64,128]{3,2,1,0:T(8,128)S(1)}, f32[2,4,64,128]{3,2,1,0:T(8,128)S(1)}, u32[]{:S(2)}, u32[]{:S(2)}) %collective-permute-start.13) | collective-permute-done | bytes 262176 | tf_op jit(solution)/shard_map/ppermute | solution.py:489
  138.3 1.3 shard_map.174
  139.6 5.8 %collective-permute-start.14 = (f32[1024,128]{1,0:T(8,128)}, f32[1024,128]{1,0:T(8,128)S(1)}, u32[]{:S(2)}, u32[]{:S(2)}) collective-permute-start(f32[1024,128]{1,0:T(8,128)} %get-tuple-element.81), channel_id=1, source_target_pairs={{0,1},{1,2},{2,3},{3,4},{4,5},{5,6},{6,7},{7,8},{8,9},{9,10},{10,1... | collective-permute-start | bytes 1572872 | tf_op jit(solution)/shard_map/ppermute | solution.py:488
  145.4 1.9 %collective-permute-start.15 = (f32[1024,128]{1,0:T(8,128)}, f32[1024,128]{1,0:T(8,128)}, u32[]{:S(2)}, u32[]{:S(2)}) collective-permute-start(f32[1024,128]{1,0:T(8,128)} %get-tuple-element.82), channel_id=1, source_target_pairs={{1,0},{2,1},{3,2},{4,3},{5,4},{6,5},{7,6},{8,7},{9,8},{10,9},{11,1... | collective-permute-start | bytes 1572872 | tf_op jit(solution)/shard_map/ppermute | solution.py:489
  147.3 17.7 %all-to-all-start.2 = ((f32[256,1,128]{2,1,0:T(1,128)}), f32[256,1,128]{2,1,0:T(1,128)}, u32[]{:S(2)}, u32[]{:S(2)}) async-start(f32[256,1,128]{2,1,0:T(1,128)} %bitcast.17), calls=%async_computation.2 | async-start | bytes 262144 | tf_op jit(solution)/shard_map/all_to_all | solution.py:494
  165.1 3.2 %shard_map.175.al = f32[2,4,128,128]{3,2,1,0:T(8,128)S(1)} custom-call(f32[2,4,128,128]{3,2,1,0:T(8,128)S(1)} %get-tuple-element.78.refs_0_.f.w1, f32[4,8]{1,0:T(4,128)S(1)} %copy-done.43, s32[4]{0:T(128)S(1)} %copy-done.44, f32[128,128]{1,0:T(8,128)S(1)} %copy-done.2, bf16[256,256]{1,0:T(8,128)(2,1)S(1)} %copy-done.3, bf16[256,256]{1,0:T(8,128)(2,1)S(1)} %copy-done.4), custom_call_target="tpu_custom_call" | custom-call | tf_op jit(solution)/shard_map/pallas_call | solution.py:470
  169.1 1.0 copy-done.34
  170.2 7.8 %shard_map.176.y2 = f32[2,4,128,128]{3,2,1,0:T(8,128)S(1)} custom-call(f32[2,4,128,128]{3,2,1,0:T(8,128)S(1)} %get-tuple-element.78.refs_0_.f.w1, f32[2,4,64,128]{3,2,1,0:T(8,128)S(1)} %copy-done.18, f32[2,4,64,128]{3,2,1,0:T(8,128)S(1)} %copy-done.20, f32[1024,128]{1,0:T(8,128)S(1)} %copy-done.34, f32[1024,128]{1,0:T(8,128)} %collective-permute-done.15.got_e, ...), custom_call_target="tpu_custom_call" | custom-call | tf_op jit(solution)/shard_map/pallas_call | solution.py:470
  178.6 1.0 copy-done.26
  179.7 1.0 copy-done.28
  180.7 2.7 %shard_map.177 = (f32[2,4,128,128]{3,2,1,0:T(8,128)}, f32[2,4,128,128]{3,2,1,0:T(8,128)}, f32[2,4,128,128]{3,2,1,0:T(8,128)}) custom-call(f32[2,4,128,128]{3,2,1,0:T(8,128)S(1)} %get-tuple-element.56.refs_0_.f.refs_1_.s0, f32[2,4,128,128]{3,2,1,0:T(8,128)S(1)} %get-tuple-element.57.refs_2_.y0, f32[2,4,128,128]{3,2,1,0:T(8,128)S(1)} %get-tuple-element.67.refs_5_.y1, ...), custom_call_target="tpu_custom_call" | custom-call | tf_op jit(solution)/shard_map/pallas_call | solution.py:470
  (106 shorter events, 9.4 us)
Async XLA Ops:
  1.7 6.2 %copy-start.2 = (f32[128,128]{1,0:T(8,128)S(1)}, f32[128,128]{1,0:T(8,128)}, u32[]{:S(2)}) copy-start(f32[128,128]{1,0:T(8,128)} %constant.18.clone.refs_7_.refs_13_.refs_3_.den) | copy-start | bytes 196612
  1.7 6.2 %copy-start.3 = (bf16[256,256]{1,0:T(8,128)(2,1)S(1)}, bf16[256,256]{1,0:T(8,128)(2,1)}, u32[]{:S(2)}) copy-start(bf16[256,256]{1,0:T(8,128)(2,1)} %constant.19.clone.refs_8_.refs_4_) | copy-start | bytes 393220
  1.7 6.2 %copy-start.4 = (bf16[256,256]{1,0:T(8,128)(2,1)S(1)}, bf16[256,256]{1,0:T(8,128)(2,1)}, u32[]{:S(2)}) copy-start(bf16[256,256]{1,0:T(8,128)(2,1)} %constant.20.clone.refs_9_.refs_5_) | copy-start | bytes 393220
  1.7 6.2 %copy-start.40 = (f32[16,16,16]{2,1,0:T(8,128)S(1)}, f32[16,16,16]{2,1,0:T(8,128)}, u32[]{:S(2)}) copy-start(f32[16,16,16]{2,1,0:T(8,128)} %param.20) | copy-start | bytes 49156
  2.5 10.7 %collective-permute-start = (f32[2,4,64,128]{3,2,1,0:T(8,128)S(1)}, f32[2,4,64,128]{3,2,1,0:T(8,128)S(1)}, u32[]{:S(2)}, u32[]{:S(2)}) collective-permute-start(f32[2,4,64,128]{3,2,1,0:T(8,128)S(1)} %get-tuple-element.44), channel_id=1, source_target_pairs={{0,16},{16,32},{32,48},{48,64},{64,80},{80,96},{96,112},{112,128},... | collective-permute-start | bytes 786440 | tf_op jit(solution)/shard_map/ppermute | solution.py:488
  6.5 1.4 copy-start.43
  6.6 8.8 %collective-permute-start.1 = (f32[2,4,64,128]{3,2,1,0:T(8,128)S(1)}, f32[2,4,64,128]{3,2,1,0:T(8,128)S(1)}, u32[]{:S(2)}, u32[]{:S(2)}) collective-permute-start(f32[2,4,64,128]{3,2,1,0:T(8,128)S(1)} %get-tuple-element.45), channel_id=1, source_target_pairs={{16,0},{32,16},{48,32},{64,48},{80,64},{96,80},{112,96},{128,112},... | collective-permute-start | bytes 786440 | tf_op jit(solution)/shard_map/ppermute | solution.py:489
  13.2 3.5 %copy-start.31 = (f32[2,4,128,128]{3,2,1,0:T(8,128)}, f32[2,4,128,128]{3,2,1,0:T(8,128)S(1)}, u32[]{:S(2)}) copy-start(f32[2,4,128,128]{3,2,1,0:T(8,128)S(1)} %get-tuple-element.50.refs_5_) | copy-start | bytes 1572868
  13.2 41.0 %copy-start.15 = (f32[4,128,128]{2,1,0:T(8,128)}, f32[4,128,128]{2,1,0:T(8,128)S(1)}, u32[]{:S(2)}) copy-start(f32[4,128,128]{2,1,0:T(8,128)S(1)} %get-tuple-element.53.refs_8_) | copy-start | bytes 786436
  15.4 38.9 %copy-start.1 = (f32[2,4,128,128]{3,2,1,0:T(8,128)S(1)}, f32[2,4,128,128]{3,2,1,0:T(8,128)}, u32[]{:S(2)}) copy-start(f32[2,4,128,128]{3,2,1,0:T(8,128)} %refs_0_.7) | copy-start | bytes 1572868
  15.4 38.9 %copy-start.7 = (bf16[256,256]{1,0:T(8,128)(2,1)S(1)}, bf16[256,256]{1,0:T(8,128)(2,1)}, u32[]{:S(2)}) copy-start(bf16[256,256]{1,0:T(8,128)(2,1)} %constant.23.clone.refs_16_.rh) | copy-start | bytes 393220
  15.4 38.9 %copy-start.8 = (bf16[256,256]{1,0:T(8,128)(2,1)S(1)}, bf16[256,256]{1,0:T(8,128)(2,1)}, u32[]{:S(2)}) copy-start(bf16[256,256]{1,0:T(8,128)(2,1)} %constant.24.clone.refs_17_.rl) | copy-start | bytes 393220
  15.4 38.9 %copy-start.9 = (bf16[256,256]{1,0:T(8,128)(2,1)S(1)}, bf16[256,256]{1,0:T(8,128)(2,1)}, u32[]{:S(2)}) copy-start(bf16[256,256]{1,0:T(8,128)(2,1)} %constant.25.clone.refs_18_.ch) | copy-start | bytes 393220
  15.4 38.9 %copy-start.11 = (bf16[256,256]{1,0:T(8,128)(2,1)S(1)}, bf16[256,256]{1,0:T(8,128)(2,1)}, u32[]{:S(2)}) copy-start(bf16[256,256]{1,0:T(8,128)(2,1)} %constant.26.clone.refs_19_.cl) | copy-start | bytes 393220
  16.7 37.5 %collective-permute-start.2 = (f32[1040,128]{1,0:T(8,128)}, f32[1040,128]{1,0:T(8,128)}, u32[]{:S(2)}, u32[]{:S(2)}) collective-permute-start(f32[1040,128]{1,0:T(8,128)} %get-tuple-element.48), channel_id=1, source_target_pairs={{0,1},{1,2},{2,3},{3,4},{4,5},{5,6},{6,7},{7,8},{8,9},{9,10},{10,1... | collective-permute-start | bytes 1597448 | tf_op jit(solution)/shard_map/ppermute | solution.py:488
  22.0 32.3 %collective-permute-start.3 = (f32[1040,128]{1,0:T(8,128)}, f32[1040,128]{1,0:T(8,128)}, u32[]{:S(2)}, u32[]{:S(2)}) collective-permute-start(f32[1040,128]{1,0:T(8,128)} %get-tuple-element.49), channel_id=1, source_target_pairs={{1,0},{2,1},{3,2},{4,3},{5,4},{6,5},{7,6},{8,7},{9,8},{10,9},{11,1... | collective-permute-start | bytes 1597448 | tf_op jit(solution)/shard_map/ppermute | solution.py:489
  23.9 30.4 %copy-start.5 = (bf16[256,256]{1,0:T(8,128)(2,1)S(1)}, bf16[256,256]{1,0:T(8,128)(2,1)}, u32[]{:S(2)}) copy-start(bf16[256,256]{1,0:T(8,128)(2,1)} %constant.21.clone.refs_14_.fh) | copy-start | bytes 393220
  23.9 30.4 %copy-start.6 = (bf16[256,256]{1,0:T(8,128)(2,1)S(1)}, bf16[256,256]{1,0:T(8,128)(2,1)}, u32[]{:S(2)}) copy-start(bf16[256,256]{1,0:T(8,128)(2,1)} %constant.22.clone.refs_15_.fl) | copy-start | bytes 393220
  23.9 29.6 %all-to-all-start = ((f32[256,1,128]{2,1,0:T(1,128)}), f32[256,1,128]{2,1,0:T(1,128)S(1)}, u32[]{:S(2)}, u32[]{:S(2)}) async-start(f32[256,1,128]{2,1,0:T(1,128)} %bitcast.3), calls=%async_computation | async-start | bytes 262144 | tf_op jit(solution)/shard_map/all_to_all | solution.py:494
  40.7 4.6 %collective-permute-start.4 = (f32[16,128]{1,0:T(8,128)S(1)}, f32[16,128]{1,0:T(8,128)S(1)}, u32[]{:S(2)}, u32[]{:S(2)}) collective-permute-start(f32[16,128]{1,0:T(8,128)S(1)} %get-tuple-element.51), channel_id=1, source_target_pairs={{0,16},{16,32},{32,48},{48,64},{64,80},{80,96},{96,112},{112,128},... | collective-permute-start | bytes 24584 | tf_op jit(solution)/shard_map/ppermute | solution.py:488
  44.0 4.7 %collective-permute-start.5 = (f32[16,128]{1,0:T(8,128)S(1)}, f32[16,128]{1,0:T(8,128)S(1)}, u32[]{:S(2)}, u32[]{:S(2)}) collective-permute-start(f32[16,128]{1,0:T(8,128)S(1)} %get-tuple-element.52), channel_id=1, source_target_pairs={{16,0},{32,16},{48,32},{64,48},{80,64},{96,80},{112,96},{128,112},... | collective-permute-start | bytes 24584 | tf_op jit(solution)/shard_map/ppermute | solution.py:489
  66.2 6.9 %copy-start.37 = (f32[4,128,128]{2,1,0:T(8,128)}, f32[4,128,128]{2,1,0:T(8,128)S(1)}, u32[]{:S(2)}) copy-start(f32[4,128,128]{2,1,0:T(8,128)S(1)} %get-tuple-element.73.refs_10_) | copy-start | bytes 786436
  66.2 6.9 %copy-start.41 = (f32[256,128]{1,0:T(8,128)}, f32[256,128]{1,0:T(8,128)S(1)}, u32[]{:S(2)}) copy-start(f32[256,128]{1,0:T(8,128)S(1)} %get-tuple-element.75) | copy-start | bytes 393220
  66.2 6.9 %copy-start.45 = (f32[4,8,128]{2,1,0:T(8,128)}, f32[4,8,128]{2,1,0:T(8,128)S(1)}, u32[]{:S(2)}) copy-start(f32[4,8,128]{2,1,0:T(8,128)S(1)} %get-tuple-element.72.refs_9_) | copy-start | bytes 49156
  66.2 6.9 %copy-start.47 = (f32[8,128]{1,0:T(8,128)}, f32[8,128]{1,0:T(8,128)S(1)}, u32[]{:S(2)}) copy-start(f32[8,128]{1,0:T(8,128)S(1)} %get-tuple-element.74.refs_12_) | copy-start | bytes 12292
  66.2 7.0 %collective-permute-start.6 = (f32[2,4,64,128]{3,2,1,0:T(8,128)S(1)}, f32[2,4,64,128]{3,2,1,0:T(8,128)S(1)}, u32[]{:S(2)}, u32[]{:S(2)}) collective-permute-start(f32[2,4,64,128]{3,2,1,0:T(8,128)S(1)} %get-tuple-element.58), channel_id=1, source_target_pairs={{0,16},{16,32},{32,48},{48,64},{64,80},{80,96},{96,112},{112,128},... | collective-permute-start | bytes 786440 | tf_op jit(solution)/shard_map/ppermute | solution.py:488
  68.3 8.4 %collective-permute-start.7 = (f32[2,4,64,128]{3,2,1,0:T(8,128)S(1)}, f32[2,4,64,128]{3,2,1,0:T(8,128)S(1)}, u32[]{:S(2)}, u32[]{:S(2)}) collective-permute-start(f32[2,4,64,128]{3,2,1,0:T(8,128)S(1)} %get-tuple-element.59), channel_id=1, source_target_pairs={{16,0},{32,16},{48,32},{64,48},{80,64},{96,80},{112,96},{128,112},... | collective-permute-start | bytes 786440 | tf_op jit(solution)/shard_map/ppermute | solution.py:489
  73.2 4.9 %copy-start.29 = (f32[2,4,128,128]{3,2,1,0:T(8,128)}, f32[2,4,128,128]{3,2,1,0:T(8,128)S(1)}, u32[]{:S(2)}) copy-start(f32[2,4,128,128]{3,2,1,0:T(8,128)S(1)} %get-tuple-element.64.al) | copy-start | bytes 1572868
  76.7 1.3 copy-start.13
  78.1 29.4 %collective-permute-start.8 = (f32[1040,128]{1,0:T(8,128)}, f32[1040,128]{1,0:T(8,128)}, u32[]{:S(2)}, u32[]{:S(2)}) collective-permute-start(f32[1040,128]{1,0:T(8,128)} %get-tuple-element.62), channel_id=1, source_target_pairs={{0,1},{1,2},{2,3},{3,4},{4,5},{5,6},{6,7},{7,8},{8,9},{9,10},{10,1... | collective-permute-start | bytes 1597448 | tf_op jit(solution)/shard_map/ppermute | solution.py:488
  82.6 24.9 %collective-permute-start.9 = (f32[1040,128]{1,0:T(8,128)}, f32[1040,128]{1,0:T(8,128)}, u32[]{:S(2)}, u32[]{:S(2)}) collective-permute-start(f32[1040,128]{1,0:T(8,128)} %get-tuple-element.63), channel_id=1, source_target_pairs={{1,0},{2,1},{3,2},{4,3},{5,4},{6,5},{7,6},{8,7},{9,8},{10,9},{11,1... | collective-permute-start | bytes 1597448 | tf_op jit(solution)/shard_map/ppermute | solution.py:489
  84.5 33.9 %all-to-all-start.1 = ((f32[256,1,128]{2,1,0:T(1,128)}), f32[256,1,128]{2,1,0:T(1,128)}, u32[]{:S(2)}, u32[]{:S(2)}) async-start(f32[256,1,128]{2,1,0:T(1,128)} %bitcast.16), calls=%async_computation.1 | async-start | bytes 262144 | tf_op jit(solution)/shard_map/all_to_all | solution.py:494
  99.4 4.6 %collective-permute-start.10 = (f32[16,128]{1,0:T(8,128)S(1)}, f32[16,128]{1,0:T(8,128)S(1)}, u32[]{:S(2)}, u32[]{:S(2)}) collective-permute-start(f32[16,128]{1,0:T(8,128)S(1)} %get-tuple-element.65), channel_id=1, source_target_pairs={{0,16},{16,32},{32,48},{48,64},{64,80},{80,96},{96,112},{112,128},... | collective-permute-start | bytes 24584 | tf_op jit(solution)/shard_map/ppermute | solution.py:488
  102.7 4.8 %collective-permute-start.11 = (f32[16,128]{1,0:T(8,128)S(1)}, f32[16,128]{1,0:T(8,128)S(1)}, u32[]{:S(2)}, u32[]{:S(2)}) collective-permute-start(f32[16,128]{1,0:T(8,128)S(1)} %get-tuple-element.66), channel_id=1, source_target_pairs={{16,0},{32,16},{48,32},{64,48},{80,64},{96,80},{112,96},{128,112},... | collective-permute-start | bytes 24584 | tf_op jit(solution)/shard_map/ppermute | solution.py:489
  127.1 12.5 %copy-start.25 = (f32[2,4,128,128]{3,2,1,0:T(8,128)}, f32[2,4,128,128]{3,2,1,0:T(8,128)S(1)}, u32[]{:S(2)}) copy-start(f32[2,4,128,128]{3,2,1,0:T(8,128)S(1)} %get-tuple-element.76.r1) | copy-start | bytes 1572868
  127.1 12.5 %copy-start.42 = (f32[256,128]{1,0:T(8,128)}, f32[256,128]{1,0:T(8,128)S(1)}, u32[]{:S(2)}) copy-start(f32[256,128]{1,0:T(8,128)S(1)} %get-tuple-element.84) | copy-start | bytes 393220
  127.1 12.5 %copy-start.49 = (f32[8,128]{1,0:T(8,128)}, f32[8,128]{1,0:T(8,128)S(1)}, u32[]{:S(2)}) copy-start(f32[8,128]{1,0:T(8,128)S(1)} %get-tuple-element.83.keep) | copy-start | bytes 12292
  127.1 7.3 %collective-permute-start.12 = (f32[2,4,64,128]{3,2,1,0:T(8,128)S(1)}, f32[2,4,64,128]{3,2,1,0:T(8,128)S(1)}, u32[]{:S(2)}, u32[]{:S(2)}) collective-permute-start(f32[2,4,64,128]{3,2,1,0:T(8,128)S(1)} %get-tuple-element.79), channel_id=1, source_target_pairs={{0,16},{16,32},{32,48},{48,64},{64,80},{80,96},{96,112},{112,128},... | collective-permute-start | bytes 786440 | tf_op jit(solution)/shard_map/ppermute | solution.py:488
  130.2 8.1 %collective-permute-start.13 = (f32[2,4,64,128]{3,2,1,0:T(8,128)S(1)}, f32[2,4,64,128]{3,2,1,0:T(8,128)S(1)}, u32[]{:S(2)}, u32[]{:S(2)}) collective-permute-start(f32[2,4,64,128]{3,2,1,0:T(8,128)S(1)} %get-tuple-element.80), channel_id=1, source_target_pairs={{16,0},{32,16},{48,32},{64,48},{80,64},{96,80},{112,96},{128,112},... | collective-permute-start | bytes 786440 | tf_op jit(solution)/shard_map/ppermute | solution.py:489
  134.4 5.2 %copy-start.17 = (f32[2,4,64,128]{3,2,1,0:T(8,128)}, f32[2,4,64,128]{3,2,1,0:T(8,128)S(1)}, u32[]{:S(2)}) copy-start(f32[2,4,64,128]{3,2,1,0:T(8,128)S(1)} %collective-permute-done.12.refs_1_.got_n) | copy-start | bytes 786436
  138.3 1.3 copy-start.19
  139.6 28.7 %collective-permute-start.14 = (f32[1024,128]{1,0:T(8,128)}, f32[1024,128]{1,0:T(8,128)S(1)}, u32[]{:S(2)}, u32[]{:S(2)}) collective-permute-start(f32[1024,128]{1,0:T(8,128)} %get-tuple-element.81), channel_id=1, source_target_pairs={{0,1},{1,2},{2,3},{3,4},{4,5},{5,6},{6,7},{7,8},{8,9},{9,10},{10,1... | collective-permute-start | bytes 1572872 | tf_op jit(solution)/shard_map/ppermute | solution.py:488
  145.4 23.7 %collective-permute-start.15 = (f32[1024,128]{1,0:T(8,128)}, f32[1024,128]{1,0:T(8,128)}, u32[]{:S(2)}, u32[]{:S(2)}) collective-permute-start(f32[1024,128]{1,0:T(8,128)} %get-tuple-element.82), channel_id=1, source_target_pairs={{1,0},{2,1},{3,2},{4,3},{5,4},{6,5},{7,6},{8,7},{9,8},{10,9},{11,1... | collective-permute-start | bytes 1572872 | tf_op jit(solution)/shard_map/ppermute | solution.py:489
  147.3 30.6 %all-to-all-start.2 = ((f32[256,1,128]{2,1,0:T(1,128)}), f32[256,1,128]{2,1,0:T(1,128)}, u32[]{:S(2)}, u32[]{:S(2)}) async-start(f32[256,1,128]{2,1,0:T(1,128)} %bitcast.17), calls=%async_computation.2 | async-start | bytes 262144 | tf_op jit(solution)/shard_map/all_to_all | solution.py:494
  165.0 4.1 %copy-start.10 = (bf16[256,256]{1,0:T(8,128)(2,1)S(1)}, bf16[256,256]{1,0:T(8,128)(2,1)}, u32[]{:S(2)}) copy-start(bf16[256,256]{1,0:T(8,128)(2,1)} %constant.25.clone.refs_18_.ch) | copy-start | bytes 393220
  165.1 4.1 %copy-start.12 = (bf16[256,256]{1,0:T(8,128)(2,1)S(1)}, bf16[256,256]{1,0:T(8,128)(2,1)}, u32[]{:S(2)}) copy-start(bf16[256,256]{1,0:T(8,128)(2,1)} %constant.26.clone.refs_19_.cl) | copy-start | bytes 393220
  165.1 4.0 %copy-start.18 = (f32[2,4,64,128]{3,2,1,0:T(8,128)S(1)}, f32[2,4,64,128]{3,2,1,0:T(8,128)}, u32[]{:S(2)}) copy-start(f32[2,4,64,128]{3,2,1,0:T(8,128)} %copy-done.17) | copy-start | bytes 786436
  165.1 4.0 %copy-start.20 = (f32[2,4,64,128]{3,2,1,0:T(8,128)S(1)}, f32[2,4,64,128]{3,2,1,0:T(8,128)}, u32[]{:S(2)}) copy-start(f32[2,4,64,128]{3,2,1,0:T(8,128)} %copy-done.19) | copy-start | bytes 786436
  (23 other events, 20.3 us)

commit v2 on v1

v2 whole, which is shorter than its diff:
```python
import math

import numpy as np

import jax
import jax.numpy as jnp
from jax import lax
from jax.experimental import pallas as pl
from jax.experimental.pallas import tpu as pltpu
from jax.sharding import PartitionSpec as P

SUB = 128
HALF = 64
VARS = 2
TIERS = 4
SLABS = VARS * TIERS
SHIFT_C = 0.5
SINK_C = 0.05
HIGH = lax.Precision.HIGHEST
F32 = jnp.float32
BF16 = jnp.bfloat16
BOTH = ("rows", "cols")
EXT = 2 * SUB


MARG = SLABS * HALF


def _doubled(mat):
    mat = np.asarray(mat, np.float32)
    top = mat.astype(BF16)
    low = (mat - top.astype(np.float32)).astype(BF16)
    return np.concatenate([np.concatenate([top, low], 1)] * 2, 0)


def _constants():
    n = np.arange(1, SUB + 1, dtype=np.float64)
    ang = math.pi / (SUB + 1)
    s = math.sqrt(2.0 / (SUB + 1)) * np.sin(ang * n[:, None] * n[None, :])
    ev = 2.0 - 2.0 * np.cos(ang * n)
    den = (ev[:, None] + ev[None, :] + SHIFT_C).astype(np.float32)
    turned = np.roll(s, HALF, axis=0)
    return [jnp.asarray(a) for a in (den, _doubled(s), _doubled(turned), _doubled(turned.T))]


def _mm(x, mat):
    xh = x.astype(BF16)
    xl = (x - xh.astype(F32)).astype(BF16)
    both = jnp.dot(jnp.concatenate([xh, xl], axis=1), mat, preferred_element_type=F32)
    return both[:, :SUB] + both[:, SUB:]


def _iota(shape, dim):
    return lax.broadcasted_iota(jnp.int32, shape, dim)


def _left(rows):
    return _iota((rows, SUB), 1) < HALF


def _tier_scalars(table, tiers):
    rows = []
    for t in range(TIERS):
        pick = tiers[t]
        rows.append([table[pick, m] for m in range(table.shape[1])])
    return rows


def _mean(row):
    total = row[0]
    for value in row[1:]:
        total = total + value
    return total * (1.0 / len(row))


def _parts(x, size=SUB):
    return [x[i : i + size] for i in range(0, x.shape[0], size)]


def _interleave(works):
    live = []
    works = list(works)
    while works or live:
        if works:
            live.append(works.pop(0))
        for work in list(live):
            try:
                next(work)
            except StopIteration:
                live.remove(work)


def _aligned_tier(t, f, dinv, mat, al):
    x = _mm(jnp.concatenate([f[v, t] for v in range(VARS)], axis=0), mat)
    yield
    x = _mm(jnp.concatenate([p.T for p in _parts(x)], axis=0), mat)
    yield
    x = _mm(x * jnp.concatenate([dinv] * VARS, axis=0), mat)
    yield
    x = _mm(jnp.concatenate([p.T for p in _parts(x)], axis=0), mat)
    yield
    for v, p in enumerate(_parts(x)):
        al[v, t] = p


def _align_all(f, rows, den, mat, al):
    _interleave(_aligned_tier(t, f, 1.0 / (_mean(rows[t]) * den[...]), mat[...], al) for t in range(TIERS))


def _column_edges(get, count, col):
    lane = _iota((SUB, SUB), 1)
    acc = jnp.zeros((SUB, SUB), F32)
    for k in range(count):
        rolled = pltpu.roll(get(k), (k - col) % SUB, 1)
        acc = jnp.where(lane == k, rolled, acc)
    return acc.T[:16]


def _row(values, ref):
    lane = _iota(ref.shape, 1)
    row = jnp.zeros(ref.shape, F32)
    for k, value in enumerate(values):
        row = jnp.where(lane == k, value, row)
    ref[...] = row


def _gathered(w_ref, gath_ref):
    return jnp.dot(w_ref[...], gath_ref[...], precision=HIGH, preferred_element_type=F32)


def _take(arr, row, lane):
    hit = (_iota(arr.shape, 0) == row) & (_iota(arr.shape, 1) == lane)
    return jnp.sum(jnp.where(hit, arr, 0.0))


def _ratio(arr, dist):
    return arr / pltpu.roll(arr, arr.shape[1] - dist, 1)


def _send_rows(s, send_n, send_s):
    for v in range(VARS):
        for t in range(TIERS):
            at = (v * TIERS + t) * HALF
            send_n[at : at + HALF, :] = s[v, t, :HALF]
            send_s[at : at + HALF, :] = s[v, t, HALF:]


def _edges(al, cond, send_n, send_s, edge_w, edge_e):
    count = SLABS if cond is None else SLABS + TIERS

    def get(k):
        return al[k // TIERS, k % TIERS] if k < SLABS else cond[k - SLABS]

    zero = jnp.zeros((16, SUB), F32)
    send_n[MARG:, :] = zero
    send_s[MARG:, :] = zero
    for k in range(count):
        x = get(k)
        send_n[MARG + k : MARG + k + 1, :] = x[0:1]
        send_s[MARG + k : MARG + k + 1, :] = x[SUB - 1 : SUB]
    edge_w[...] = _column_edges(get, count, 0)
    edge_e[...] = _column_edges(get, count, SUB - 1)


def _prepare(power, material, table, tiers, den, mat, al, cond, send_n, send_s, edge_w, edge_e, row):
    rows = _tier_scalars(table, tiers)
    for t in range(TIERS):
        ids = material[t]
        c = jnp.zeros((SUB, SUB), F32)
        for m, value in enumerate(rows[t]):
            c = jnp.where(ids == m, value, c)
        cond[t] = c
    _send_rows(power, send_n, send_s)
    _row([_dot(power, None, v) for v in range(VARS)], row)
    _align_all(power, rows, den, mat, al)
    _edges(al, cond, send_n, send_s, edge_w, edge_e)


def _weigh(n_rows, n_cols, own, slot_s, slot_v, inverse, w_out):
    total = n_rows * n_cols
    me = lax.axis_index("rows") * n_cols + lax.axis_index("cols")
    sub = _iota((8, total), 0)
    lane = _iota((8, total), 1)
    mine = jnp.full((8, total), -1, jnp.int32)
    for k, step in enumerate((0, -n_cols, n_cols, -1, 1)):
        g = jnp.minimum(jnp.maximum(me + step, 0), total - 1)
        mine = jnp.where(sub == k, slot_s[g], mine)
    picked = jnp.dot((mine == lane).astype(F32), inverse[...], precision=HIGH, preferred_element_type=F32)
    spread = (_iota((own, total), 1) % own == _iota((own, total), 0)).astype(F32)
    full = jnp.dot(picked, spread, precision=HIGH, preferred_element_type=F32)
    full = jnp.where((lane // own) == (mine // own), full, 0.0)
    place = (_iota((total, total), 0) == slot_v[...]).astype(F32)
    weights = jnp.dot(full, place, precision=HIGH, preferred_element_type=F32)
    weights = weights * (1.0 / (SUB * SUB * TIERS))
    w_out[...] = jnp.where(sub == 5, 1.0, weights)


def _ext_rows(f, got_n, got_s, v, t):
    at = (v * TIERS + t) * HALF
    x = f[v, t]
    return [x[:HALF], got_n[at : at + HALF, :], got_s[at : at + HALF, :], x[HALF:]]


def _pack(f, got_n, got_s, row, *rest):
    if len(rest) == 5:
        edge_w, edge_e, send_w, send_e, pay = rest
        send_w[TIERS * EXT :, :] = edge_w[...]
        send_e[TIERS * EXT :, :] = edge_e[...]
    else:
        send_w, send_e, pay = rest
    pay[...] = jnp.broadcast_to(row[0:1, :], pay.shape)
    left = _left(HALF)
    for t in range(TIERS):
        for part in range(4):
            at = t * EXT + part * HALF
            x0 = _ext_rows(f, got_n, got_s, 0, t)[part]
            x1 = _ext_rows(f, got_n, got_s, 1, t)[part]
            send_w[at : at + HALF, :] = jnp.where(left, x0, pltpu.roll(x1, HALF, 1))
            send_e[at : at + HALF, :] = jnp.where(left, pltpu.roll(x1, HALF, 1), x0)


def _offset_tier(t, halo, f, got_n, got_s, got_w, got_e, dinv, masks, fwd, inv, use):
    wm = got_w[t * EXT : (t + 1) * EXT, :]
    em = got_e[t * EXT : (t + 1) * EXT, :]
    left = _left(EXT)
    stack = []
    for v in range(VARS):
        mid = jnp.concatenate(_ext_rows(f, got_n, got_s, v, t), axis=0)
        before = wm if v == 0 else pltpu.roll(wm, HALF, 1)
        after = em if v == 0 else pltpu.roll(em, HALF, 1)
        stack += [jnp.where(left, mid, before), jnp.where(left, after, mid)]
    x = _mm(jnp.concatenate(stack, axis=0), fwd)
    yield
    stack = []
    for p in _parts(x, EXT):
        stack += [p[:SUB].T, p[SUB:].T]
    x = _mm(jnp.concatenate(stack, axis=0), fwd)
    yield
    has_n, has_w = masks
    quarter = [dinv * (has_w * has_n), dinv * has_w, dinv * has_n, dinv]
    x = _mm(x * jnp.concatenate(quarter * VARS, axis=0), inv)
    yield
    left = _left(SUB)
    stack = []
    parts = _parts(x)
    for i in range(0, len(parts), 2):
        stack.append(jnp.where(left, parts[i], parts[i + 1]).T)
        if halo:
            other = jnp.where(left, parts[i + 1], parts[i]).T
            stack += [other[:8], other[SUB - 8 :]]
    x = _mm(jnp.concatenate(stack, axis=0), inv)
    yield
    parts = _parts(x, SUB + 16 if halo else SUB)
    for v in range(VARS):
        a, b = parts[2 * v : 2 * v + 2]
        tile = jnp.where(left, a[:SUB], b[:SUB])
        if halo:
            use(v, t, tile, jnp.where(_left(16), a[SUB:], b[SUB:]), jnp.where(left, b[:SUB], a[:SUB]))
        else:
            use(v, t, tile, None, None)


def _masks():
    return (jnp.where(lax.axis_index("rows") > 0, 1.0, 0.0), jnp.where(lax.axis_index("cols") > 0, 1.0, 0.0))


def _solve(f, got_n, got_s, got_w, got_e, al, rows, den, fwd, inv, y, y_rows, y_cols):
    cols = _side_columns(got_w, got_e)
    low = _iota((16, SUB), 0) < 8

    def use(v, t, tile, ends, side):
        k = v * TIERS + t
        y[v, t] = tile + al[v, t]
        at = MARG + k
        y_rows[v, t] = ends + jnp.where(low, got_s[at : at + 1, :], got_n[at : at + 1, :])
        y_cols[v, t] = side + _column_pair(cols, k)

    _interleave(
        _offset_tier(t, True, f, got_n, got_s, got_w, got_e, 1.0 / (_mean(rows[t]) * den[...]), _masks(),
                     fwd[...], inv[...], use)
        for t in range(TIERS)
    )
    return cols


def _side_columns(got_w, got_e):
    base = TIERS * EXT
    pad = jnp.zeros((SUB - 32, SUB), F32)
    return jnp.concatenate([got_w[base:, :], got_e[base:, :], pad], axis=0).T


def _column_pair(cols, k):
    west = pltpu.roll(cols, SUB - 1 - k, 1)
    east = pltpu.roll(cols, SUB - 16 - k, 1)
    return jnp.where(_left(SUB), east, west)


def _shifts(x, ends, side):
    sub = _iota((SUB, SUB), 0)
    lane = _iota((SUB, SUB), 1)
    north = jnp.where(sub == 0, ends[15:16, :], pltpu.roll(x, 1, 0))
    south = jnp.where(sub == SUB - 1, ends[0:1, :], pltpu.roll(x, SUB - 1, 0))
    west = pltpu.roll(jnp.where(lane == SUB - 1, side, x), 1, 1)
    east = pltpu.roll(jnp.where(lane == 0, side, x), SUB - 1, 1)
    return north, south, west, east


def _inside(n_rows, n_cols):
    r = lax.axis_index("rows")
    c = lax.axis_index("cols")
    one = jnp.float32(1.0)
    zero = jnp.float32(0.0)
    return (
        jnp.where(r > 0, one, zero),
        jnp.where(r < n_rows - 1, one, zero),
        jnp.where(c > 0, one, zero),
        jnp.where(c < n_cols - 1, one, zero),
    )


def _operate(z, z_rows, z_cols, cond, c_rows, c_cols, out):
    for t in range(TIERS):
        c = cond[t]
        coefs = [0.5 * (c + n) for n in _shifts(c, c_rows[t], c_cols[t])]
        for v in range(VARS):
            u = z[v, t]
            around = _shifts(u, z_rows[v, t], z_cols[v, t])
            acc = coefs[0] * (u - around[0])
            for k in range(1, 4):
                acc = acc + coefs[k] * (u - around[k])
            if t + 1 < TIERS:
                acc = acc + (c + cond[t + 1]) * (u - z[v, t + 1])
            if t > 0:
                acc = acc - (cond[t - 1] + c) * (z[v, t - 1] - u)
            if t == 0:
                acc = acc + SINK_C * c * u
            out[v, t] = acc


def _dot(a, b, v):
    total = jnp.zeros((SUB, SUB), F32)
    for t in range(TIERS):
        total = total + (a[v, t] * b[v, t] if b is not None else a[v, t])
    return jnp.sum(total)


def _around(y_rows, y_cols, e, base, v, inside):
    north, south, west, east = [_take(e, k, base + v) for k in range(1, 5)]
    low = _iota((16, SUB), 0) < 8
    left = _left(SUB)
    return (
        jnp.where(low, (y_rows + south) * inside[1], (y_rows + north) * inside[0]),
        jnp.where(left, (y_cols + east) * inside[3], (y_cols + west) * inside[2]),
    )


def _begin(n_rows, n_cols, power, got_n, got_s, got_w, got_e, al, cond, w_ref, gath, table, tiers, den, mat, fwd, inv,
           y, y_rows, y_cols, s, al_s, send_n, send_s, edge_w, edge_e, row, c_rows, c_cols, e_out, z, z_rows, z_cols):
    rows = _tier_scalars(table, tiers)
    cols = _solve(power, got_n, got_s, got_w, got_e, al, rows, den, fwd, inv, y, y_rows, y_cols)
    low = _iota((16, SUB), 0) < 8
    for t in range(TIERS):
        at = MARG + SLABS + t
        c_rows[t] = jnp.where(low, got_s[at : at + 1, :], got_n[at : at + 1, :])
        c_cols[t] = _column_pair(cols, SLABS + t)
    e = _gathered(w_ref, gath)
    e_out[...] = e
    inside = _inside(n_rows, n_cols)
    for v in range(VARS):
        own = _take(e, 0, v)
        for t in range(TIERS):
            z[v, t] = y[v, t] + own
            z_rows[v, t], z_cols[v, t] = _around(y_rows[v, t], y_cols[v, t], e, 0, v, inside)
    _operate(z, z_rows, z_cols, cond, c_rows, c_cols, s)
    _send_rows(s, send_n, send_s)
    _align_all(s, rows, den, mat, al_s)
    _edges(al_s, None, send_n, send_s, edge_w, edge_e)
    _row(
        [_dot(power, z, v) for v in range(VARS)]
        + [_dot(z, s, v) for v in range(VARS)]
        + [_dot(s, None, v) for v in range(VARS)],
        row,
    )


def _step(n_rows, n_cols, power, s0, got_n, got_s, got_w, got_e, al, y0, y0_rows, y0_cols, cond, c_rows, c_cols,
          w_ref, e0, gath, table, tiers, den, fwd, inv,
          y1, r1, z1, w1, send_n, send_s, row, keep, y1_rows, y1_cols, z_rows, z_cols):
    rows = _tier_scalars(table, tiers)
    _solve(s0, got_n, got_s, got_w, got_e, al, rows, den, fwd, inv, y1, y1_rows, y1_cols)
    res = _gathered(w_ref, gath)
    quotient = _ratio(res, 2)
    alphas = [_take(quotient, 5, v) for v in range(VARS)]
    lane = _iota(res.shape, 1)
    moved = pltpu.roll(res, res.shape[1] - 4, 1)
    e1 = e0[...] - jnp.where(lane == 0, alphas[0], alphas[1]) * moved
    inside = _inside(n_rows, n_cols)
    for v in range(VARS):
        own = _take(e1, 0, v)
        a = alphas[v]
        for t in range(TIERS):
            r1[v, t] = power[v, t] - a * s0[v, t]
            z1[v, t] = (y0[v, t] - a * y1[v, t]) + own
            z_rows[v, t], z_cols[v, t] = _around(
                y0_rows[v, t] - a * y1_rows[v, t], y0_cols[v, t] - a * y1_cols[v, t], e1, 0, v, inside
            )
    _operate(z1, z_rows, z_cols, cond, c_rows, c_cols, w1)
    _send_rows(w1, send_n, send_s)
    _row(
        [_dot(r1, z1, v) for v in range(VARS)]
        + [_dot(z1, w1, v) for v in range(VARS)]
        + [_dot(z1, s0, v) for v in range(VARS)]
        + [_dot(w1, None, v) for v in range(VARS)],
        row,
    )
    kept = []
    for values in ((res, 5, 0), (res, 5, 2), None, (e0[...], 0, 0), (res, 0, 4)):
        kept += alphas if values is None else [_take(values[0], values[1], values[2] + v) for v in range(VARS)]
    _row(kept, keep)


def _align_last(f, table, tiers, den, mat, al):
    _align_all(f, _tier_scalars(table, tiers), den, mat, al)


def _finish(s0, y0, y1, r1, z1, w1, got_n, got_s, got_w, got_e, al, w_ref, keep, gath, table, tiers, den, fwd, inv,
            x_out, r_out, z_out):
    rows = _tier_scalars(table, tiers)
    res = _gathered(w_ref, gath)
    k = keep[...]
    values = []
    for v in range(VARS):
        def wide(value):
            return jnp.full((8, SUB), 1.0, F32) * value

        rz0, d0, a0, e0, cs = [_take(k, 0, 2 * j + v) for j in range(5)]
        rz1, d1, zs = [_take(res, 5, 2 * j + v) for j in range(3)]
        cw = _take(res, 0, 6 + v)
        beta_w = wide(rz1) / wide(rz0)
        below = wide(d1) + 2.0 * beta_w * wide(zs) + beta_w * beta_w * wide(d0)
        alpha = _take(wide(rz1) / below, 0, 0)
        beta = _take(beta_w, 0, 0)
        values.append((a0, e0, alpha, beta, -alpha * (cw + beta * cs)))

    def use(v, t, tile, ends, side):
        a0, e0, alpha, beta, change = values[v]
        z = z1[v, t]
        first = y0[v, t] + e0
        x_out[v, t] = a0 * first + alpha * (z + beta * first)
        r_out[v, t] = r1[v, t] - alpha * (w1[v, t] + beta * s0[v, t])
        z_out[v, t] = (z - alpha * ((tile + al[v, t]) + beta * y1[v, t])) + change

    _interleave(
        _offset_tier(t, False, w1, got_n, got_s, got_w, got_e, 1.0 / (_mean(rows[t]) * den[...]), _masks(),
                     fwd[...], inv[...], use)
        for t in range(TIERS)
    )


def _call(body, outs, args, smem=(), scratch=()):
    specs = [
        pl.BlockSpec(memory_space=pltpu.SMEM if i in smem else pltpu.VMEM) for i in range(len(args))
    ]
    return pl.pallas_call(
        body,
        out_shape=[jax.ShapeDtypeStruct(s, F32) for s in outs],
        in_specs=specs,
        out_specs=[pl.BlockSpec(memory_space=pltpu.VMEM) for _ in outs],
        scratch_shapes=[pltpu.VMEM(s, F32) for s in scratch],
        compiler_params=pltpu.CompilerParams(vmem_limit_bytes=VMEM_LIMIT),
    )(*args)


VMEM_LIMIT = 16 << 20
FIELD = (VARS, TIERS, SUB, SUB)
ENDS = (VARS, TIERS, 16, SUB)
EDGE = (16, SUB)
ROW = (8, SUB)
TIER_FIELD = (TIERS, SUB, SUB)
MARGIN = (MARG + 16, SUB)
BARE_MARGIN = (MARG, SUB)
SIDE = (TIERS * EXT + 16, SUB)
BARE_SIDE = (TIERS * EXT, SUB)


def _exchange(first, second, axis):
    count = lax.axis_size(axis)
    before = lax.ppermute(second, axis, [(i, i + 1) for i in range(count - 1)])
    after = lax.ppermute(first, axis, [(i + 1, i) for i in range(count - 1)])
    return before, after


def _everywhere(pay):
    return lax.all_to_all(pay, BOTH, 0, 0, tiled=True)


def shards(power, material, cond_table, tier_table, coarse_slot, coarse_inverse):
    n_rows = lax.axis_size("rows")
    n_cols = lax.axis_size("cols")
    total = n_rows * n_cols
    own = coarse_inverse.shape[1]
    den, mat, fwd, inv = _constants()
    pay_shape = (total, SUB)

    (weights,) = _call(
        lambda *refs: _weigh(n_rows, n_cols, own, *refs),
        [(8, total)],
        [coarse_slot, coarse_slot.reshape(1, total), coarse_inverse.reshape(total, own)],
        smem=(0,),
    )
    al, cond, send_n, send_s, edge_w, edge_e, row = _call(
        _prepare,
        [FIELD, TIER_FIELD, MARGIN, MARGIN, EDGE, EDGE, ROW],
        [power, material, cond_table, tier_table, den, mat],
        smem=(2, 3),
    )
    got_n, got_s = _exchange(send_n, send_s, "rows")
    send_w, send_e, pay = _call(_pack, [SIDE, SIDE, pay_shape], [power, got_n, got_s, row, edge_w, edge_e])
    got_w, got_e = _exchange(send_w, send_e, "cols")
    gath = _everywhere(pay)
    y0, y0_rows, y0_cols, s0, al, send_n, send_s, edge_w, edge_e, row, c_rows, c_cols, e0 = _call(
        lambda *refs: _begin(n_rows, n_cols, *refs),
        [FIELD, ENDS, FIELD, FIELD, FIELD, MARGIN, MARGIN, EDGE, EDGE, ROW, (TIERS, 16, SUB), TIER_FIELD, ROW],
        [power, got_n, got_s, got_w, got_e, al, cond, weights, gath, cond_table, tier_table, den, mat, fwd, inv],
        smem=(9, 10),
        scratch=(FIELD, ENDS, FIELD),
    )

    got_n, got_s = _exchange(send_n, send_s, "rows")
    send_w, send_e, pay = _call(_pack, [SIDE, SIDE, pay_shape], [s0, got_n, got_s, row, edge_w, edge_e])
    got_w, got_e = _exchange(send_w, send_e, "cols")
    gath = _everywhere(pay)
    y1, r1, z1, w1, send_n, send_s, row, keep = _call(
        lambda *refs: _step(n_rows, n_cols, *refs),
        [FIELD, FIELD, FIELD, FIELD, BARE_MARGIN, BARE_MARGIN, ROW, ROW],
        [power, s0, got_n, got_s, got_w, got_e, al, y0, y0_rows, y0_cols, cond, c_rows, c_cols,
         weights, e0, gath, cond_table, tier_table, den, fwd, inv],
        smem=(16, 17),
        scratch=(ENDS, FIELD, ENDS, FIELD),
    )

    got_n, got_s = _exchange(send_n, send_s, "rows")
    (al,) = _call(_align_last, [FIELD], [w1, cond_table, tier_table, den, mat], smem=(1, 2))
    send_w, send_e, pay = _call(_pack, [BARE_SIDE, BARE_SIDE, pay_shape], [w1, got_n, got_s, row])
    got_w, got_e = _exchange(send_w, send_e, "cols")
    gath = _everywhere(pay)
    return tuple(
        _call(
            _finish,
            [FIELD, FIELD, FIELD],
            [s0, y0, y1, r1, z1, w1, got_n, got_s, got_w, got_e, al, weights, keep, gath,
             cond_table, tier_table, den, fwd, inv],
            smem=(14, 15),
        )
    )


def solution(mesh):
    in_specs = (P(None, None, "rows", "cols"), P(None, "rows", "cols"), P(), P(), P(), P())
    out_specs = (P(None, None, "rows", "cols"),) * 3
    return jax.shard_map(shards, mesh=mesh, in_specs=in_specs, out_specs=out_specs, check_vma=False)
```

time: 185 us -> 168 us (0.908)
  starting transfers between devices: 93 us -> 60.1 us
  blocking collectives: 0 us -> 24.1 us
  Pallas kernels: 45.3 us -> 23.8 us
  waiting for transfers between devices: 24.3 us -> 44.4 us
  local copies, waits for them, and re-layouts: 19.7 us -> 14 us
    all_to_all x0 -> x1, blocking collectives: none -> 24.1 us  [_everywhere(): return lax.all_to_all(pay, BOTH, 0, 0, tiled=True)]
    pallas_call x12 -> x9, Pallas kernels: 45.3 us -> 23.8 us  [_call(): pl.pallas_call(body, out_shape=[jax.ShapeDtypeStruct(s, F32) for s in out...]
    all_to_all x3 -> x2, starting transfers between devices: 49.4 us -> 28.2 us  [_everywhere(): return lax.all_to_all(pay, BOTH, 0, 0, tiled=True)]
    all_to_all x3 -> x2, waiting for transfers between devices: 4.88 us -> 22.2 us  [_everywhere(): return lax.all_to_all(pay, BOTH, 0, 0, tiled=True)]
    ppermute x8 -> x6, starting transfers between devices: 31.2 us -> 22.3 us  [_exchange(): before = lax.ppermute(second, axis, [(i, i + 1) for i in range(count - 1)])]
    ppermute x8 -> x6, waiting for transfers between devices: 2.94 us -> 10.6 us  [_exchange(): before = lax.ppermute(second, axis, [(i, i + 1) for i in range(count - 1)])]
    unnamed x104 -> x50, local copies, waits for them, and re-layouts: 19.7 us -> 14 us
    ppermute x8 -> x6, waiting for transfers between devices: 16.4 us -> 11.6 us  [_exchange(): after = lax.ppermute(first, axis, [(i + 1, i) for i in range(count - 1)])]
  transfers between devices with their start and end apart: 19 -> 14, of which waited for: 7 -> 8; matrix products, arithmetic and copies ran while one was open for 0% -> 0% of each run, Pallas kernels for 14% -> 2%
where the time goes in v2:
time: 168 us; the launch traced here: 167 us
  starting transfers between devices  60.1 us (36%)
  waiting for transfers between devices  44.4 us (26%)
  blocking collectives  24.1 us (14%)
  Pallas kernels  23.8 us (14%)
  local copies, waits for them, and re-layouts  14 us (8%)
    all_to_all x2, starting transfers between devices, _everywhere(): return lax.all_to_all(pay, BOTH, 0, 0, tiled=True)  28.2 us
    all_to_all x1, blocking collectives, _everywhere(): return lax.all_to_all(pay, BOTH, 0, 0, tiled=True)  24.1 us
    pallas_call x9, Pallas kernels, _call(): pl.pallas_call(body, out_shape=[jax.ShapeDtypeStruct(s, F32) for s in out...  23.8 us
    ppermute x6, starting transfers between devices, _exchange(): before = lax.ppermute(second, axis, [(i, i + 1) for i in range(count - 1)])  22.3 us
    all_to_all x2, waiting for transfers between devices, _everywhere(): return lax.all_to_all(pay, BOTH, 0, 0, tiled=True)  22.2 us
    unnamed x50, local copies, waits for them, and re-layouts  14 us
    ppermute x6, waiting for transfers between devices, _exchange(): after = lax.ppermute(first, axis, [(i + 1, i) for i in range(count - 1)])  11.6 us
    ppermute x6, waiting for transfers between devices, _exchange(): before = lax.ppermute(second, axis, [(i, i + 1) for i in range(count - 1)])  10.6 us
  transfers between devices with their start and end apart: 14, of which 8 were waited for; matrix products, arithmetic and copies ran while one was open for 0% of the time, Pallas kernels for 2%

profile of v2, /device:TPU:1, one launch (start us, length us, event | category | flops | bytes accessed | tf_op | source)
XLA Modules:
  0.0 167.3 jit_solution(995257998601513188)
XLA Ops:
  0.6 1.0 copy-done
  1.7 0.8 copy-done.2
  2.5 0.9 copy-done.6
  3.4 0.9 copy-done.18
  4.4 0.7 copy-done.20
  5.1 0.7 copy-done.22
  5.7 2.1 %shard_map.121 = (f32[2,4,128,128]{3,2,1,0:T(8,128)S(1)}, f32[4,128,128]{2,1,0:T(8,128)S(1)}, f32[528,128]{1,0:T(8,128)S(1)}, f32[528,128]{1,0:T(8,128)S(1)}, f3...) custom-call(f32[2,4,128,128]{3,2,1,0:T(8,128)S(1)} %copy-done, s32[4,128,128]{2,1,0:T(8,128)S(1)} %copy-done.18, ...), custom_call_target="tpu_custom_call" | custom-call | tf_op jit(solution)/shard_map/pallas_call | solution.py:464
  7.8 0.8 copy-done.16
  8.7 4.0 %collective-permute-start = (f32[528,128]{1,0:T(8,128)S(1)}, f32[528,128]{1,0:T(8,128)S(1)}, u32[]{:S(2)}, u32[]{:S(2)}) collective-permute-start(f32[528,128]{1,0:T(8,128)S(1)} %get-tuple-element.40), channel_id=1, source_target_pairs={{0,16},{16,32},{32,48},{48,64},{64,80},{80,96},{96,112},{112,128},... | collective-permute-start | bytes 811016 | tf_op jit(solution)/shard_map/ppermute | solution.py:488
  12.7 1.3 collective-permute-start.1
  14.0 3.8 %collective-permute-done.got_n.refs_1_ = f32[528,128]{1,0:T(8,128)S(1)} collective-permute-done((f32[528,128]{1,0:T(8,128)S(1)}, f32[528,128]{1,0:T(8,128)S(1)}, u32[]{:S(2)}, u32[]{:S(2)}) %collective-permute-start) | collective-permute-done | bytes 270368 | tf_op jit(solution)/shard_map/ppermute | solution.py:488
  17.8 3.8 %collective-permute-done.1.got_s.refs_2_ = f32[528,128]{1,0:T(8,128)S(1)} collective-permute-done((f32[528,128]{1,0:T(8,128)S(1)}, f32[528,128]{1,0:T(8,128)S(1)}, u32[]{:S(2)}, u32[]{:S(2)}) %collective-permute-start.1) | collective-permute-done | bytes 270368 | tf_op jit(solution)/shard_map/ppermute | solution.py:489
  21.7 1.2 shard_map.122
  22.9 5.2 %collective-permute-start.2 = (f32[1040,128]{1,0:T(8,128)}, f32[1040,128]{1,0:T(8,128)S(1)}, u32[]{:S(2)}, u32[]{:S(2)}) collective-permute-start(f32[1040,128]{1,0:T(8,128)} %get-tuple-element.45), channel_id=1, source_target_pairs={{0,1},{1,2},{2,3},{3,4},{4,5},{5,6},{6,7},{7,8},{8,9},{9,10},{10,1... | collective-permute-start | bytes 1597448 | tf_op jit(solution)/shard_map/ppermute | solution.py:488
  28.2 1.9 %collective-permute-start.3 = (f32[1040,128]{1,0:T(8,128)}, f32[1040,128]{1,0:T(8,128)}, u32[]{:S(2)}, u32[]{:S(2)}) collective-permute-start(f32[1040,128]{1,0:T(8,128)} %get-tuple-element.46), channel_id=1, source_target_pairs={{1,0},{2,1},{3,2},{4,3},{5,4},{6,5},{7,6},{8,7},{9,8},{10,9},{11,1... | collective-permute-start | bytes 1597448 | tf_op jit(solution)/shard_map/ppermute | solution.py:489
  30.1 16.8 %all-to-all-start = ((f32[256,1,128]{2,1,0:T(1,128)}), f32[256,1,128]{2,1,0:T(1,128)S(1)}, u32[]{:S(2)}, u32[]{:S(2)}) async-start(f32[256,1,128]{2,1,0:T(1,128)} %bitcast.3), calls=%async_computation | async-start | bytes 262144 | tf_op jit(solution)/shard_map/all_to_all | solution.py:494
  46.9 0.7 copy-done.24
  47.6 1.0 shard_map.123.refs_7_.refs_13_.w_ref
  48.6 11.1 %all-to-all-done = f32[256,1,128]{2,1,0:T(1,128)S(1)} async-done(((f32[256,1,128]{2,1,0:T(1,128)}), f32[256,1,128]{2,1,0:T(1,128)S(1)}, u32[]{:S(2)}, u32[]{:S(2)}) %all-to-all-start) | async-done | bytes 131104 | tf_op jit(solution)/shard_map/all_to_all | solution.py:494
  59.8 0.8 copy-done.8
  60.6 0.6 copy-done.21
  61.3 1.0 copy-done.9
  62.3 1.0 copy-done.17
  63.4 5.8 %shard_map.124 = (f32[2,4,128,128]{3,2,1,0:T(8,128)S(1)}, f32[2,4,16,128]{3,2,1,0:T(8,128)S(1)}, f32[2,4,128,128]{3,2,1,0:T(8,128)S(1)}, f32[2,4,128,128]{3,2,1,...) custom-call(f32[2,4,128,128]{3,2,1,0:T(8,128)S(1)} %copy-done.1, ...), custom_call_target="tpu_custom_call" | custom-call | tf_op jit(solution)/shard_map/pallas_call | solution.py:464
  69.2 2.0 %collective-permute-start.4 = (f32[528,128]{1,0:T(8,128)S(1)}, f32[528,128]{1,0:T(8,128)S(1)}, u32[]{:S(2)}, u32[]{:S(2)}) collective-permute-start(f32[528,128]{1,0:T(8,128)S(1)} %get-tuple-element.52), channel_id=1, source_target_pairs={{0,16},{16,32},{32,48},{48,64},{64,80},{80,96},{96,112},{112,128},... | collective-permute-start | bytes 811016 | tf_op jit(solution)/shard_map/ppermute | solution.py:488
  71.2 1.3 collective-permute-start.5
  72.5 3.5 %collective-permute-done.4.got_n.refs_2_ = f32[528,128]{1,0:T(8,128)S(1)} collective-permute-done((f32[528,128]{1,0:T(8,128)S(1)}, f32[528,128]{1,0:T(8,128)S(1)}, u32[]{:S(2)}, u32[]{:S(2)}) %collective-permute-start.4) | collective-permute-done | bytes 270368 | tf_op jit(solution)/shard_map/ppermute | solution.py:488
  76.0 3.8 %collective-permute-done.5.got_s.refs_3_ = f32[528,128]{1,0:T(8,128)S(1)} collective-permute-done((f32[528,128]{1,0:T(8,128)S(1)}, f32[528,128]{1,0:T(8,128)S(1)}, u32[]{:S(2)}, u32[]{:S(2)}) %collective-permute-start.5) | collective-permute-done | bytes 270368 | tf_op jit(solution)/shard_map/ppermute | solution.py:489
  79.9 0.2 shard_map.125
  80.1 4.5 %collective-permute-start.6 = (f32[1040,128]{1,0:T(8,128)S(1)}, f32[1040,128]{1,0:T(8,128)S(1)}, u32[]{:S(2)}, u32[]{:S(2)}) collective-permute-start(f32[1040,128]{1,0:T(8,128)S(1)} %get-tuple-element.57), channel_id=1, source_target_pairs={{0,1},{1,2},{2,3},{3,4},{4,5},{5,6},{6,7},{7,8},{8,9},{9,10},{10,1... | collective-permute-start | bytes 1597448 | tf_op jit(solution)/shard_map/ppermute | solution.py:488
  84.6 1.9 %collective-permute-start.7 = (f32[1040,128]{1,0:T(8,128)S(1)}, f32[1040,128]{1,0:T(8,128)S(1)}, u32[]{:S(2)}, u32[]{:S(2)}) collective-permute-start(f32[1040,128]{1,0:T(8,128)S(1)} %get-tuple-element.58), channel_id=1, source_target_pairs={{1,0},{2,1},{3,2},{4,3},{5,4},{6,5},{7,6},{8,7},{9,8},{10,9},{11,1... | collective-permute-start | bytes 1597448 | tf_op jit(solution)/shard_map/ppermute | solution.py:489
  86.5 24.1 %all_to_all.33 = f32[256,1,128]{2,1,0:T(1,128)S(1)} all-to-all(f32[256,1,128]{2,1,0:T(1,128)S(1)} %bitcast.18), channel_id=1, replica_groups=mesh['rows'=16,'cols'=16] {'rows','cols'}, dimensions={0} | all-to-all | bytes 262144 | tf_op jit(solution)/shard_map/all_to_all | solution.py:494
  110.6 5.0 %shard_map.126 = (f32[2,4,128,128]{3,2,1,0:T(8,128)S(1)}, f32[2,4,128,128]{3,2,1,0:T(8,128)S(1)}, f32[2,4,128,128]{3,2,1,0:T(8,128)S(1)}, f32[2,4,128,128]{3,2,1...) custom-call(f32[2,4,128,128]{3,2,1,0:T(8,128)S(1)} %copy-done.1, ...), custom_call_target="tpu_custom_call" | custom-call | tf_op jit(solution)/shard_map/pallas_call | solution.py:464
  115.7 0.8 copy-done.14
  116.4 2.0 %collective-permute-start.8 = (f32[512,128]{1,0:T(8,128)S(1)}, f32[512,128]{1,0:T(8,128)S(1)}, u32[]{:S(2)}, u32[]{:S(2)}) collective-permute-start(f32[512,128]{1,0:T(8,128)S(1)} %get-tuple-element.70), channel_id=1, source_target_pairs={{0,16},{16,32},{32,48},{48,64},{64,80},{80,96},{96,112},{112,128},... | collective-permute-start | bytes 786440 | tf_op jit(solution)/shard_map/ppermute | solution.py:488
  118.5 1.3 collective-permute-start.9
  119.8 3.3 %collective-permute-done.8.got_n = f32[512,128]{1,0:T(8,128)S(1)} collective-permute-done((f32[512,128]{1,0:T(8,128)S(1)}, f32[512,128]{1,0:T(8,128)S(1)}, u32[]{:S(2)}, u32[]{:S(2)}) %collective-permute-start.8) | collective-permute-done | bytes 262176 | tf_op jit(solution)/shard_map/ppermute | solution.py:488
  123.1 3.8 %collective-permute-done.9.got_s = f32[512,128]{1,0:T(8,128)S(1)} collective-permute-done((f32[512,128]{1,0:T(8,128)S(1)}, f32[512,128]{1,0:T(8,128)S(1)}, u32[]{:S(2)}, u32[]{:S(2)}) %collective-permute-start.9) | collective-permute-done | bytes 262176 | tf_op jit(solution)/shard_map/ppermute | solution.py:489
  126.9 1.2 shard_map.127
  128.2 4.5 %collective-permute-start.10 = (f32[1024,128]{1,0:T(8,128)}, f32[1024,128]{1,0:T(8,128)}, u32[]{:S(2)}, u32[]{:S(2)}) collective-permute-start(f32[1024,128]{1,0:T(8,128)} %get-tuple-element.73), channel_id=1, source_target_pairs={{0,1},{1,2},{2,3},{3,4},{4,5},{5,6},{6,7},{7,8},{8,9},{9,10},{10,1... | collective-permute-start | bytes 1572872 | tf_op jit(solution)/shard_map/ppermute | solution.py:488
  132.7 1.9 %collective-permute-start.11 = (f32[1024,128]{1,0:T(8,128)}, f32[1024,128]{1,0:T(8,128)}, u32[]{:S(2)}, u32[]{:S(2)}) collective-permute-start(f32[1024,128]{1,0:T(8,128)} %get-tuple-element.74), channel_id=1, source_target_pairs={{1,0},{2,1},{3,2},{4,3},{5,4},{6,5},{7,6},{8,7},{9,8},{10,9},{11,1... | collective-permute-start | bytes 1572872 | tf_op jit(solution)/shard_map/ppermute | solution.py:489
  134.6 11.4 %all-to-all-start.2 = ((f32[256,1,128]{2,1,0:T(1,128)}), f32[256,1,128]{2,1,0:T(1,128)S(1)}, u32[]{:S(2)}, u32[]{:S(2)}) async-start(f32[256,1,128]{2,1,0:T(1,128)} %bitcast.9), calls=%async_computation.2 | async-start | bytes 262144 | tf_op jit(solution)/shard_map/all_to_all | solution.py:494
  146.0 1.8 %shard_map.128.al = f32[2,4,128,128]{3,2,1,0:T(8,128)S(1)} custom-call(f32[2,4,128,128]{3,2,1,0:T(8,128)S(1)} %get-tuple-element.69.f.w1, f32[4,8]{1,0:T(4,128)S(1)} %copy-done.21, s32[4]{0:T(128)S(1)} %copy-done.23, f32[128,128]{1,0:T(8,128)S(1)} %copy-done.3, bf16[256,256]{1,0:T(8,128)(2,1)S(1)} %copy-done.7), custom_call_target="tpu_custom_call" | custom-call | tf_op jit(solution)/shard_map/pallas_call | solution.py:464
  147.8 11.1 %all-to-all-done.2 = f32[256,1,128]{2,1,0:T(1,128)S(1)} async-done(((f32[256,1,128]{2,1,0:T(1,128)}), f32[256,1,128]{2,1,0:T(1,128)S(1)}, u32[]{:S(2)}, u32[]{:S(2)}) %all-to-all-start.2) | async-done | bytes 131104 | tf_op jit(solution)/shard_map/all_to_all | solution.py:494
  159.0 1.0 copy-done.11
  160.0 1.0 copy-done.13
  161.0 1.0 copy-done.15
  162.1 5.3 %shard_map.129 = (f32[2,4,128,128]{3,2,1,0:T(8,128)}, f32[2,4,128,128]{3,2,1,0:T(8,128)}, f32[2,4,128,128]{3,2,1,0:T(8,128)}) custom-call(f32[2,4,128,128]{3,2,1,0:T(8,128)S(1)} %get-tuple-element.50.f.refs_1_.s0, f32[2,4,128,128]{3,2,1,0:T(8,128)S(1)} %get-tuple-element.51.refs_7_.y0, f32[2,4,128,128]{3,2,1,0:T(8,128)S(1)} %copy-done.11, ...), custom_call_target="tpu_custom_call" | custom-call | tf_op jit(solution)/shard_map/pallas_call | solution.py:464
  (40 shorter events, 0.1 us)
Async XLA Ops:
  0.6 1.0 copy-start
  1.7 0.8 copy-start.2
  2.5 0.9 copy-start.6
  3.4 0.9 copy-start.18
  4.4 0.7 copy-start.20
  5.1 0.7 copy-start.22
  7.8 0.8 copy-start.16
  8.7 9.2 %collective-permute-start = (f32[528,128]{1,0:T(8,128)S(1)}, f32[528,128]{1,0:T(8,128)S(1)}, u32[]{:S(2)}, u32[]{:S(2)}) collective-permute-start(f32[528,128]{1,0:T(8,128)S(1)} %get-tuple-element.40), channel_id=1, source_target_pairs={{0,16},{16,32},{32,48},{48,64},{64,80},{80,96},{96,112},{112,128},... | collective-permute-start | bytes 811016 | tf_op jit(solution)/shard_map/ppermute | solution.py:488
  12.7 9.0 %collective-permute-start.1 = (f32[528,128]{1,0:T(8,128)S(1)}, f32[528,128]{1,0:T(8,128)S(1)}, u32[]{:S(2)}, u32[]{:S(2)}) collective-permute-start(f32[528,128]{1,0:T(8,128)S(1)} %get-tuple-element.41), channel_id=1, source_target_pairs={{16,0},{32,16},{48,32},{64,48},{80,64},{96,80},{112,96},{128,112},... | collective-permute-start | bytes 811016 | tf_op jit(solution)/shard_map/ppermute | solution.py:489
  21.7 25.3 %copy-start.19 = (f32[16,16,16]{2,1,0:T(8,128)S(1)}, f32[16,16,16]{2,1,0:T(8,128)}, u32[]{:S(2)}) copy-start(f32[16,16,16]{2,1,0:T(8,128)} %param.15) | copy-start | bytes 49156
  21.7 38.9 %copy-start.1 = (f32[2,4,128,128]{3,2,1,0:T(8,128)S(1)}, f32[2,4,128,128]{3,2,1,0:T(8,128)}, u32[]{:S(2)}) copy-start(f32[2,4,128,128]{3,2,1,0:T(8,128)} %refs_0_.5) | copy-start | bytes 1572868
  21.7 38.9 %copy-start.7 = (bf16[256,256]{1,0:T(8,128)(2,1)S(1)}, bf16[256,256]{1,0:T(8,128)(2,1)}, u32[]{:S(2)}) copy-start(bf16[256,256]{1,0:T(8,128)(2,1)} %constant.9.clone.mat.refs_12_) | copy-start | bytes 393220
  22.9 36.8 %collective-permute-start.2 = (f32[1040,128]{1,0:T(8,128)}, f32[1040,128]{1,0:T(8,128)S(1)}, u32[]{:S(2)}, u32[]{:S(2)}) collective-permute-start(f32[1040,128]{1,0:T(8,128)} %get-tuple-element.45), channel_id=1, source_target_pairs={{0,1},{1,2},{2,3},{3,4},{4,5},{5,6},{6,7},{7,8},{8,9},{9,10},{10,1... | collective-permute-start | bytes 1597448 | tf_op jit(solution)/shard_map/ppermute | solution.py:488
  28.2 32.4 %collective-permute-start.3 = (f32[1040,128]{1,0:T(8,128)}, f32[1040,128]{1,0:T(8,128)}, u32[]{:S(2)}, u32[]{:S(2)}) collective-permute-start(f32[1040,128]{1,0:T(8,128)} %get-tuple-element.46), channel_id=1, source_target_pairs={{1,0},{2,1},{3,2},{4,3},{5,4},{6,5},{7,6},{8,7},{9,8},{10,9},{11,1... | collective-permute-start | bytes 1597448 | tf_op jit(solution)/shard_map/ppermute | solution.py:489
  30.1 30.5 %copy-start.4 = (bf16[256,256]{1,0:T(8,128)(2,1)S(1)}, bf16[256,256]{1,0:T(8,128)(2,1)}, u32[]{:S(2)}) copy-start(bf16[256,256]{1,0:T(8,128)(2,1)} %constant.11.clone.refs_14_.refs_20_.inv) | copy-start | bytes 393220
  30.1 30.5 %copy-start.5 = (bf16[256,256]{1,0:T(8,128)(2,1)S(1)}, bf16[256,256]{1,0:T(8,128)(2,1)}, u32[]{:S(2)}) copy-start(bf16[256,256]{1,0:T(8,128)(2,1)} %constant.10.clone.refs_13_.refs_19_.fwd) | copy-start | bytes 393220
  30.1 29.6 %all-to-all-start = ((f32[256,1,128]{2,1,0:T(1,128)}), f32[256,1,128]{2,1,0:T(1,128)S(1)}, u32[]{:S(2)}, u32[]{:S(2)}) async-start(f32[256,1,128]{2,1,0:T(1,128)} %bitcast.3), calls=%async_computation | async-start | bytes 262144 | tf_op jit(solution)/shard_map/all_to_all | solution.py:494
  46.9 0.7 copy-start.24
  47.6 13.1 %copy-start.3 = (f32[128,128]{1,0:T(8,128)S(1)}, f32[128,128]{1,0:T(8,128)}, u32[]{:S(2)}) copy-start(f32[128,128]{1,0:T(8,128)} %constant.8.clone.den.refs_11_.refs_18_) | copy-start | bytes 196612
  59.8 0.8 copy-start.8
  60.6 0.7 copy-start.21
  60.6 0.7 copy-start.23
  61.3 1.0 copy-start.9
  62.3 1.0 copy-start.17
  69.2 6.8 %collective-permute-start.4 = (f32[528,128]{1,0:T(8,128)S(1)}, f32[528,128]{1,0:T(8,128)S(1)}, u32[]{:S(2)}, u32[]{:S(2)}) collective-permute-start(f32[528,128]{1,0:T(8,128)S(1)} %get-tuple-element.52), channel_id=1, source_target_pairs={{0,16},{16,32},{32,48},{48,64},{64,80},{80,96},{96,112},{112,128},... | collective-permute-start | bytes 811016 | tf_op jit(solution)/shard_map/ppermute | solution.py:488
  71.2 8.6 %collective-permute-start.5 = (f32[528,128]{1,0:T(8,128)S(1)}, f32[528,128]{1,0:T(8,128)S(1)}, u32[]{:S(2)}, u32[]{:S(2)}) collective-permute-start(f32[528,128]{1,0:T(8,128)S(1)} %get-tuple-element.53), channel_id=1, source_target_pairs={{16,0},{32,16},{48,32},{64,48},{80,64},{96,80},{112,96},{128,112},... | collective-permute-start | bytes 811016 | tf_op jit(solution)/shard_map/ppermute | solution.py:489
  80.1 30.6 %collective-permute-start.6 = (f32[1040,128]{1,0:T(8,128)S(1)}, f32[1040,128]{1,0:T(8,128)S(1)}, u32[]{:S(2)}, u32[]{:S(2)}) collective-permute-start(f32[1040,128]{1,0:T(8,128)S(1)} %get-tuple-element.57), channel_id=1, source_target_pairs={{0,1},{1,2},{2,3},{3,4},{4,5},{5,6},{6,7},{7,8},{8,9},{9,10},{10,1... | collective-permute-start | bytes 1597448 | tf_op jit(solution)/shard_map/ppermute | solution.py:488
  84.6 26.1 %collective-permute-start.7 = (f32[1040,128]{1,0:T(8,128)S(1)}, f32[1040,128]{1,0:T(8,128)S(1)}, u32[]{:S(2)}, u32[]{:S(2)}) collective-permute-start(f32[1040,128]{1,0:T(8,128)S(1)} %get-tuple-element.58), channel_id=1, source_target_pairs={{1,0},{2,1},{3,2},{4,3},{5,4},{6,5},{7,6},{8,7},{9,8},{10,9},{11,1... | collective-permute-start | bytes 1597448 | tf_op jit(solution)/shard_map/ppermute | solution.py:489
  115.6 0.8 copy-start.14
  116.4 11.7 %copy-start.10 = (f32[2,4,128,128]{3,2,1,0:T(8,128)}, f32[2,4,128,128]{3,2,1,0:T(8,128)S(1)}, u32[]{:S(2)}) copy-start(f32[2,4,128,128]{3,2,1,0:T(8,128)S(1)} %get-tuple-element.66.y1) | copy-start | bytes 1572868
  116.4 11.7 %copy-start.12 = (f32[2,4,128,128]{3,2,1,0:T(8,128)}, f32[2,4,128,128]{3,2,1,0:T(8,128)S(1)}, u32[]{:S(2)}) copy-start(f32[2,4,128,128]{3,2,1,0:T(8,128)S(1)} %get-tuple-element.67.r1) | copy-start | bytes 1572868
  116.4 6.6 %collective-permute-start.8 = (f32[512,128]{1,0:T(8,128)S(1)}, f32[512,128]{1,0:T(8,128)S(1)}, u32[]{:S(2)}, u32[]{:S(2)}) collective-permute-start(f32[512,128]{1,0:T(8,128)S(1)} %get-tuple-element.70), channel_id=1, source_target_pairs={{0,16},{16,32},{32,48},{48,64},{64,80},{80,96},{96,112},{112,128},... | collective-permute-start | bytes 786440 | tf_op jit(solution)/shard_map/ppermute | solution.py:488
  118.5 8.4 %collective-permute-start.9 = (f32[512,128]{1,0:T(8,128)S(1)}, f32[512,128]{1,0:T(8,128)S(1)}, u32[]{:S(2)}, u32[]{:S(2)}) collective-permute-start(f32[512,128]{1,0:T(8,128)S(1)} %get-tuple-element.71), channel_id=1, source_target_pairs={{16,0},{32,16},{48,32},{64,48},{80,64},{96,80},{112,96},{128,112},... | collective-permute-start | bytes 786440 | tf_op jit(solution)/shard_map/ppermute | solution.py:489
  128.2 30.8 %collective-permute-start.10 = (f32[1024,128]{1,0:T(8,128)}, f32[1024,128]{1,0:T(8,128)}, u32[]{:S(2)}, u32[]{:S(2)}) collective-permute-start(f32[1024,128]{1,0:T(8,128)} %get-tuple-element.73), channel_id=1, source_target_pairs={{0,1},{1,2},{2,3},{3,4},{4,5},{5,6},{6,7},{7,8},{8,9},{9,10},{10,1... | collective-permute-start | bytes 1572872 | tf_op jit(solution)/shard_map/ppermute | solution.py:488
  132.7 26.3 %collective-permute-start.11 = (f32[1024,128]{1,0:T(8,128)}, f32[1024,128]{1,0:T(8,128)}, u32[]{:S(2)}, u32[]{:S(2)}) collective-permute-start(f32[1024,128]{1,0:T(8,128)} %get-tuple-element.74), channel_id=1, source_target_pairs={{1,0},{2,1},{3,2},{4,3},{5,4},{6,5},{7,6},{8,7},{9,8},{10,9},{11,1... | collective-permute-start | bytes 1572872 | tf_op jit(solution)/shard_map/ppermute | solution.py:489
  134.6 24.4 %all-to-all-start.2 = ((f32[256,1,128]{2,1,0:T(1,128)}), f32[256,1,128]{2,1,0:T(1,128)S(1)}, u32[]{:S(2)}, u32[]{:S(2)}) async-start(f32[256,1,128]{2,1,0:T(1,128)} %bitcast.9), calls=%async_computation.2 | async-start | bytes 262144 | tf_op jit(solution)/shard_map/all_to_all | solution.py:494
  158.9 1.0 copy-start.11
  160.0 1.0 copy-start.13
  161.0 1.0 copy-start.15
